TPU v7x, 32 devices: a whole 2x2x4 slice. The times are simulated.
32 devices in a mesh: seg: 8 (over z, y), ctl: 4 (over x, core).
Axes of the slice: x: 2, y: 2, z: 4, core: 2. Of those that a mesh axis runs over, the one named last changes fastest.
Arguments:
- transition: float32 [8, 1024, 1024], P('seg'), may hold values from -1 to 1
- control_map: float32 [8, 1024, 256], P('seg'), may hold values from -1.5 to 1.5
- weights: float32 [8, 1024], P('seg'), may hold values from 0.01 to 0.5
Outputs:
- sensitivity: float32 [8, 1024, 2048], P('seg', None, 'ctl')
- hessian_tiles: float32 [4, 512, 512], P('ctl', 'seg')
All inputs are finite; a program needn't handle non-finite values.
Results may differ from a plain program's by a relative error of at most 0.0003.
Values sent between devices are 32-bit elements; how exact they have to be, the bound alone decides.
No kernel may reach another device: no remote copies, remote signals or barrier semaphores. Data moves between devices by JAX's collectives and lax.ppermute only.
A program may use at most 128 MiB of HBM per device.

v0:
```python
import functools

import jax
import jax.numpy as jnp
from jax import lax
from jax.experimental import pallas as pl
from jax.experimental.pallas import tpu as pltpu
from jax.sharding import PartitionSpec as P


F32, BF16 = jnp.float32, jnp.bfloat16
VMEM = pl.BlockSpec(memory_space=pltpu.VMEM)


def size_of(shape, dtype):
    total = jnp.dtype(dtype).itemsize
    for dim in shape:
        total *= dim
    return total


def call(kernel, outs, *args, scratch=(), flops=0, extra=4 << 20):
    moved = sum(size_of(a.shape, a.dtype) for a in args) + sum(size_of(o.shape, o.dtype) for o in outs)
    used = moved + sum(size_of(m.shape, m.dtype) for m in scratch) + extra
    return pl.pallas_call(
        kernel,
        out_shape=outs,
        in_specs=[VMEM] * len(args),
        out_specs=[VMEM] * len(outs),
        scratch_shapes=scratch,
        cost_estimate=pl.CostEstimate(flops=flops, bytes_accessed=moved, transcendentals=0),
        compiler_params=pltpu.CompilerParams(vmem_limit_bytes=min(used, 60 << 20)),
    )(*args)


def out(shape, dtype=F32):
    return jax.ShapeDtypeStruct(shape, dtype)


def split(value):
    high = value.astype(BF16)
    return high, (value - high.astype(F32)).astype(BF16)


def split_kernel(trans_ref, control_ref, high_ref, low_ref, start_ref):
    rows = trans_ref.shape[0]
    for i in range(0, rows, 128):
        for k in range(0, control_ref.shape[1], 128):
            start_ref[k : k + 128, i : i + 128] = control_ref[i : i + 128, k : k + 128].T
    for i in range(0, rows, 128):
        high, low = split(trans_ref[i : i + 128, :])
        high_ref[:, i : i + 128] = high.T
        low_ref[:, i : i + 128] = low.T


def step_kernel(x_ref, high_ref, low_ref, y_ref):
    rows = x_ref.shape[0]
    high, low = split(x_ref[...])
    both = jnp.concatenate([high, low], axis=0)
    for col in range(0, y_ref.shape[1], 256):
        at = slice(col, col + 256)
        first = jnp.dot(both, high_ref[:, at], preferred_element_type=F32)
        second = jnp.dot(high, low_ref[:, at], preferred_element_type=F32)
        y_ref[:, at] = first[:rows] + (first[rows:] + second)


def gram3(left_high, left_low, right_high, right_low):
    dims = (((1,), (1,)), ((), ()))
    rows = left_high.shape[0]
    both = jnp.concatenate([left_high, left_low], axis=0)
    first = lax.dot_general(both, right_high, dims, preferred_element_type=F32)
    second = lax.dot_general(left_high, right_low, dims, preferred_element_type=F32)
    return first[:rows] + (first[rows:] + second)


class Layout:
    def __init__(self, nseg, nctl, nu, ticks):
        self.nseg, self.nctl, self.nu, self.ticks = nseg, nctl, nu, ticks
        self.stride = nseg // (2 * nctl)
        self.width = nu // nctl

    def gather(self, dst, pair, start_ref, piece_refs, limit):
        seg = lax.axis_index("seg")
        ctl = lax.axis_index("ctl")
        chip, core = ctl // 2, ctl % 2
        for b in range(2):
            age = seg - (2 * pair + b) * self.stride
            base = b * self.nu

            @pl.when((age < 0) | (age >= limit))
            def _():
                dst[base : base + self.nu, :] = jnp.zeros((self.nu, dst.shape[1]), F32)

            if start_ref is not None:

                @pl.when(age == 0)
                def _():
                    dst[base : base + self.nu, :] = start_ref[...]

            for n, tick in enumerate(self.ticks):

                @pl.when(age == tick)
                def _():
                    for r in range(self.nctl // 2):
                        for e in range(2):
                            owner = 2 * (chip ^ r) + (core ^ e)
                            at = pl.multiple_of(base + owner * self.width, self.width)
                            dst[pl.ds(at, self.width), :] = piece_refs[n * self.nctl + 2 * r + e][...]


def early_kernel(layout, weight_ref, start_ref, *refs):
    nseg, pieces = layout.nseg, len(layout.ticks) * layout.nctl
    piece_refs, out_refs = refs[:pieces], refs[pieces : pieces + nseg]
    sens, high, low, w_high, w_low, tile = refs[pieces + nseg :]
    layout.gather(sens, lax.axis_index("ctl"), start_ref, piece_refs, nseg - 2)
    for i in range(0, sens.shape[0], 128):
        at = slice(i, i + 128)
        high[at, :], low[at, :] = split(sens[at, :])
        w_high[at, :], w_low[at, :] = split(sens[at, :] * weight_ref[...])
    nu = layout.nu
    tile[:nu, :nu] = gram3(high[:nu, :], low[:nu, :], w_high[:nu, :], w_low[:nu, :])
    tile[:, nu:] = gram3(high[...], low[...], w_high[nu:, :], w_low[nu:, :])
    for i in range(0, nu, 128):
        for k in range(0, nu, 128):
            tile[nu + k : nu + k + 128, i : i + 128] = tile[i : i + 128, nu + k : nu + k + 128].T
    seg = lax.axis_index("seg")
    rows = tile.shape[0] // nseg
    for r in range(nseg):
        out_refs[r][...] = tile[pl.ds(pl.multiple_of((seg ^ r) * rows, rows), rows), :]


def late_kernel(layout, weight_ref, *refs):
    nseg, nu, width = layout.nseg, layout.nu, layout.width
    pieces = len(layout.ticks) * layout.nctl
    piece_refs, out_refs = refs[:pieces], refs[pieces:-3]
    sens, high, low = refs[-3:]
    layout.gather(sens, 0, None, piece_refs, nseg)
    seg = lax.axis_index("seg")
    own = pl.multiple_of(lax.axis_index("ctl") * width, width)
    for i in range(0, sens.shape[0], 128):
        high[i : i + 128, :], low[i : i + 128, :] = split(sens[i : i + 128, :])
    both = jnp.concatenate([sens[pl.ds(own, width), :], sens[pl.ds(own + nu, width), :]], axis=0)
    own_high, own_low = split(both * weight_ref[...])
    left = gram3(own_high, own_low, high[:nu, :], low[:nu, :])
    right = gram3(own_high, own_low, high[nu:, :], low[nu:, :])
    rows = out_refs[0].shape[0]
    last = seg == nseg - 1
    second_late = (seg - layout.stride) >= nseg - 2
    for i in range(layout.stride):
        at = slice(i * rows, (i + 1) * rows)
        to = slice(width + i * rows, width + (i + 1) * rows)
        upper = jnp.concatenate([left[at], right[at]], axis=1)
        lower = jnp.concatenate([left[to], jnp.where(second_late, right[to], 0.0)], axis=1)
        out_refs[2 * i][...] = jnp.where(last, upper, lower)
        out_refs[2 * i + 1][...] = jnp.where(last, lower, upper)


def place_kernel(layout, start_ref, *refs):
    pieces = len(layout.ticks) * layout.nctl
    piece_refs, (sens_ref, sens) = refs[:pieces], refs[pieces:]
    layout.gather(sens, lax.axis_index("ctl"), start_ref, piece_refs, layout.nseg)
    for i in range(0, sens.shape[0], 128):
        for k in range(0, sens.shape[1], 128):
            sens_ref[k : k + 128, i : i + 128] = sens[i : i + 128, k : k + 128].T


def wave_pairs(nseg, tick):
    pairs = [(i, i + 1) for i in range(tick - 1, nseg - 1)] + [(nseg - 1, tick - 1)]
    idle = tick - 1
    pairs += [(i, i ^ 1 if (i ^ 1) < idle else i) for i in range(idle)]
    return pairs


def xor_swap(value, axis, by):
    devices = lax.axis_size(axis)
    return lax.ppermute(value, axis, [(i, i ^ by) for i in range(devices)])


def local(transition, control_map, weights):
    trans = transition[0]
    nseg = lax.axis_size("seg")
    nctl = lax.axis_size("ctl")
    nx, nu = control_map.shape[1], control_map.shape[2]
    stride = nseg // (2 * nctl)
    width = nu // nctl
    rows = 2 * nu // nseg

    newest = lax.dynamic_slice_in_dim(control_map[0], lax.axis_index("ctl") * width, width, 1).T
    high, low, start = call(
        split_kernel, [out(trans.shape, BF16)] * 2 + [out((nu, nx))], trans, control_map[0]
    )

    pieces = {}
    early = None
    for tick in range(1, nseg):
        moved = lax.ppermute(newest, "seg", wave_pairs(nseg, tick))
        (newest,) = call(
            step_kernel, [out(newest.shape)], moved, high, low, flops=6 * width * nx * nx
        )
        group = []
        for r in range(nctl // 2):
            here = newest
            if r:
                here = xor_swap(newest, "ctl", 2 * r)
            there = xor_swap(here, "ctl", 1)
            group += [here, there]
        pieces[tick] = group

    def kernel_of(kernel, ticks):
        layout = Layout(nseg, nctl, nu, ticks)
        return functools.partial(kernel, layout), [p for t in ticks for p in pieces[t]]

    tall = (2 * nu, nx)
    body, given = kernel_of(early_kernel, list(range(1, nseg - 2)))
    early = call(
            body,
        [out((rows, 2 * nu))] * nseg,
        weights,
        start,
        *given,
        scratch=[pltpu.VMEM(tall, F32)] + [pltpu.VMEM(tall, BF16)] * 4 + [pltpu.VMEM((2 * nu, 2 * nu), F32)],
        flops=6 * nx * (2 * nu) ** 2,
    )
    total = early[0]
    terms = []
    for r in range(1, nseg):
        terms.append(xor_swap(early[r], "seg", r))

    late_ticks = sorted({nseg - 1 - stride, nseg - 2 - stride, nseg - 2, nseg - 1})
    body, given = kernel_of(late_kernel, late_ticks)
    late = call(
            body,
        [out((rows, 2 * nu))] * (2 * stride),
        weights,
        *given,
        scratch=[pltpu.VMEM(tall, F32)] + [pltpu.VMEM(tall, BF16)] * 2,
        flops=6 * nx * 2 * width * 2 * nu,
    )
    for i in range(stride):
        for half in range(2):
            pairs = []
            for c in range(nctl):
                near = half * (nseg // 2) + c * stride + i
                other = (1 - half) * (nseg // 2) + c * stride + i
                pairs.append(((nseg - 1) * nctl + c, near * nctl))
                pairs.append(((nseg - 2) * nctl + c, other * nctl))
            terms.append(lax.ppermute(late[2 * i + half], ("seg", "ctl"), pairs))

    body, given = kernel_of(place_kernel, list(range(1, nseg)))
    (sens,) = call(body, [out((nx, 2 * nu))], start, *given, scratch=[pltpu.VMEM(tall, F32)])
    for term in terms:
        total = total + term
    return (sens[None], total[None])


def solution(mesh):
    return jax.shard_map(
        local,
        mesh=mesh,
        in_specs=(P("seg", None, None), P("seg", None, None), P("seg", None)),
        out_specs=(P("seg", None, "ctl"), P("ctl", "seg", None)),
        check_vma=False,
    )
```

profile of v0, /device:TPU:0, one launch (start us, length us, event | category | flops | bytes accessed | tf_op | source)
XLA Modules:
  0.0 116.3 jit_solution(1615515380759224728)
XLA Ops:
  0.6 1.3 %constant_dynamic-slice_fusion = f32[1,1024,64]{2,1,0:T(8,128)S(1)} fusion(f32[1,1024,256]{2,1,0:T(8,128)} %param.4, s32[]{:T(128)S(6)} %select_n.3), kind=kLoop, calls=%fused_computation.1 | loop fusion | bytes 524292 | tf_op jit(solution)/shard_map/dynamic_slice | solution.py:188
  2.2 3.0 %collective-permute-start = (f32[64,1024]{1,0:T(8,128)S(1)}, f32[64,1024]{1,0:T(8,128)S(1)}, u32[]{:S(2)}, u32[]{:S(2)}) collective-permute-start(f32[64,1024]{1,0:T(8,128)S(1)} %bitcast.11), channel_id=1, source_target_pairs={{0,4},{4,8},{8,12},{12,16},{16,20},{20,24},{24,28},{28,0},{1,5},{5... | collective-permute-start | bytes 786440 | tf_op jit(solution)/shard_map/ppermute | solution.py:196
  5.2 2.2 %copy-done = f32[1,1024,1024]{2,1,0:T(8,128)S(1)} copy-done((f32[1,1024,1024]{2,1,0:T(8,128)S(1)}, f32[1,1024,1024]{2,1,0:T(8,128)}, u32[]{:S(2)}) %copy-start) | copy-done | bytes 4194328
  7.4 1.6 %shard_map.50 = (bf16[1024,1024]{1,0:T(8,128)(2,1)S(1)}, bf16[1024,1024]{1,0:T(8,128)(2,1)S(1)}, f32[256,1024]{1,0:T(8,128)S(1)}) custom-call(f32[1024,1024]{1,0:T(8,128)S(1)} %bitcast.8, f32[1024,256]{1,0:T(8,128)S(1)} %bitcast.9), custom_call_target="tpu_custom_call" | custom-call | bytes 10485760 | tf_op jit(solution)/shard_map/pallas_call | solution.py:25
  9.0 5.6 %collective-permute-done.x_ref = f32[64,1024]{1,0:T(8,128)S(1)} collective-permute-done((f32[64,1024]{1,0:T(8,128)S(1)}, f32[64,1024]{1,0:T(8,128)S(1)}, u32[]{:S(2)}, u32[]{:S(2)}) %collective-permute-start) | collective-permute-done | bytes 262176 | tf_op jit(solution)/shard_map/ppermute | solution.py:196
  14.6 0.8 shard_map.51.refs_0_
  15.4 0.7 collective-permute-start.4
  16.0 0.8 shard_map.52.refs_4_
  16.8 9.0 %collective-permute-start.8 = (f32[64,1024]{1,0:T(8,128)S(1)}, f32[64,1024]{1,0:T(8,128)S(1)}, u32[]{:S(2)}, u32[]{:S(2)}) collective-permute-start(f32[64,1024]{1,0:T(8,128)S(1)} %shard_map.52.refs_4_), channel_id=1, source_target_pairs={{8,12},{12,16},{16,20},{20,24},{24,28},{28,8},{0,4},{4,0},{9,13},{... | collective-permute-start | bytes 786440 | tf_op jit(solution)/shard_map/ppermute | solution.py:196
  25.8 4.7 %collective-permute-done.8.x_ref = f32[64,1024]{1,0:T(8,128)S(1)} collective-permute-done((f32[64,1024]{1,0:T(8,128)S(1)}, f32[64,1024]{1,0:T(8,128)S(1)}, u32[]{:S(2)}, u32[]{:S(2)}) %collective-permute-start.8) | collective-permute-done | bytes 262176 | tf_op jit(solution)/shard_map/ppermute | solution.py:196
  30.5 0.8 shard_map.53.refs_8_
  31.3 3.7 %collective-permute-start.12 = (f32[64,1024]{1,0:T(8,128)S(1)}, f32[64,1024]{1,0:T(8,128)S(1)}, u32[]{:S(2)}, u32[]{:S(2)}) collective-permute-start(f32[64,1024]{1,0:T(8,128)S(1)} %shard_map.53.refs_8_), channel_id=1, source_target_pairs={{12,16},{16,20},{20,24},{24,28},{28,12},{0,4},{4,0},{8,8},{13,17},... | collective-permute-start | bytes 786440 | tf_op jit(solution)/shard_map/ppermute | solution.py:196
  34.9 1.6 %collective-permute-start.2 = (f32[64,1024]{1,0:T(8,128)S(1)}, f32[64,1024]{1,0:T(8,128)S(1)}, u32[]{:S(2)}, u32[]{:S(2)}) collective-permute-start(f32[64,1024]{1,0:T(8,128)S(1)} %shard_map.51.refs_0_), channel_id=1, source_target_pairs={{0,2},{1,3},{2,0},{3,1},{4,6},{5,7},{6,4},{7,5},{8,10},{9,11},{10,... | collective-permute-start | bytes 786440 | tf_op jit(solution)/shard_map/ppermute | solution.py:176
  36.5 3.1 %collective-permute-done.12.x_ref = f32[64,1024]{1,0:T(8,128)S(1)} collective-permute-done((f32[64,1024]{1,0:T(8,128)S(1)}, f32[64,1024]{1,0:T(8,128)S(1)}, u32[]{:S(2)}, u32[]{:S(2)}) %collective-permute-start.12) | collective-permute-done | bytes 262176 | tf_op jit(solution)/shard_map/ppermute | solution.py:196
  39.7 0.8 shard_map.54.refs_12_
  40.5 2.1 %collective-permute-start.16 = (f32[64,1024]{1,0:T(8,128)S(1)}, f32[64,1024]{1,0:T(8,128)S(1)}, u32[]{:S(2)}, u32[]{:S(2)}) collective-permute-start(f32[64,1024]{1,0:T(8,128)S(1)} %shard_map.54.refs_12_), channel_id=1, source_target_pairs={{16,20},{20,24},{24,28},{28,16},{0,4},{4,0},{8,12},{12,8},{17,21},... | collective-permute-start | bytes 786440 | tf_op jit(solution)/shard_map/ppermute | solution.py:196
  42.5 1.5 %collective-permute-start.6 = (f32[64,1024]{1,0:T(8,128)S(1)}, f32[64,1024]{1,0:T(8,128)S(1)}, u32[]{:S(2)}, u32[]{:S(2)}) collective-permute-start(f32[64,1024]{1,0:T(8,128)S(1)} %shard_map.52.refs_4_), channel_id=1, source_target_pairs={{0,2},{1,3},{2,0},{3,1},{4,6},{5,7},{6,4},{7,5},{8,10},{9,11},{10,... | collective-permute-start | bytes 786440 | tf_op jit(solution)/shard_map/ppermute | solution.py:176
  44.5 2.3 %collective-permute-done.16.x_ref = f32[64,1024]{1,0:T(8,128)S(1)} collective-permute-done((f32[64,1024]{1,0:T(8,128)S(1)}, f32[64,1024]{1,0:T(8,128)S(1)}, u32[]{:S(2)}, u32[]{:S(2)}) %collective-permute-start.16) | collective-permute-done | bytes 262176 | tf_op jit(solution)/shard_map/ppermute | solution.py:196
  46.9 0.8 shard_map.55.refs_16_.refs_0_
  47.7 3.9 %collective-permute-start.20 = (f32[64,1024]{1,0:T(8,128)S(1)}, f32[64,1024]{1,0:T(8,128)S(1)}, u32[]{:S(2)}, u32[]{:S(2)}) collective-permute-start(f32[64,1024]{1,0:T(8,128)S(1)} %shard_map.55.refs_16_.refs_0_), channel_id=1, source_target_pairs={{20,24},{24,28},{28,20},{0,4},{4,0},{8,12},{12,8},{16,16},{21,25},... | collective-permute-start | bytes 786440 | tf_op jit(solution)/shard_map/ppermute | solution.py:196
  51.6 1.6 %collective-permute-start.10 = (f32[64,1024]{1,0:T(8,128)S(1)}, f32[64,1024]{1,0:T(8,128)S(1)}, u32[]{:S(2)}, u32[]{:S(2)}) collective-permute-start(f32[64,1024]{1,0:T(8,128)S(1)} %shard_map.53.refs_8_), channel_id=1, source_target_pairs={{0,2},{1,3},{2,0},{3,1},{4,6},{5,7},{6,4},{7,5},{8,10},{9,11},{10,... | collective-permute-start | bytes 786440 | tf_op jit(solution)/shard_map/ppermute | solution.py:176
  53.2 0.5 collective-permute-start.7
  53.7 0.5 collective-permute-start.14
  54.2 1.7 %collective-permute-done.20.x_ref = f32[64,1024]{1,0:T(8,128)S(1)} collective-permute-done((f32[64,1024]{1,0:T(8,128)S(1)}, f32[64,1024]{1,0:T(8,128)S(1)}, u32[]{:S(2)}, u32[]{:S(2)}) %collective-permute-start.20) | collective-permute-done | bytes 262176 | tf_op jit(solution)/shard_map/ppermute | solution.py:196
  56.0 0.8 shard_map.56.refs_20_.refs_4_
  56.8 3.0 %collective-permute-done.10.refs_10_ = f32[64,1024]{1,0:T(8,128)S(1)} collective-permute-done((f32[64,1024]{1,0:T(8,128)S(1)}, f32[64,1024]{1,0:T(8,128)S(1)}, u32[]{:S(2)}, u32[]{:S(2)}) %collective-permute-start.10) | collective-permute-done | bytes 262176 | tf_op jit(solution)/shard_map/ppermute | solution.py:176
  59.8 2.5 %collective-permute-start.18 = (f32[64,1024]{1,0:T(8,128)S(1)}, f32[64,1024]{1,0:T(8,128)S(1)}, u32[]{:S(2)}, u32[]{:S(2)}) collective-permute-start(f32[64,1024]{1,0:T(8,128)S(1)} %shard_map.55.refs_16_.refs_0_), channel_id=1, source_target_pairs={{0,2},{1,3},{2,0},{3,1},{4,6},{5,7},{6,4},{7,5},{8,10},{9,11},{10,... | collective-permute-start | bytes 786440 | tf_op jit(solution)/shard_map/ppermute | solution.py:176
  62.3 1.5 %collective-permute-done.14.refs_14_ = f32[64,1024]{1,0:T(8,128)S(1)} collective-permute-done((f32[64,1024]{1,0:T(8,128)S(1)}, f32[64,1024]{1,0:T(8,128)S(1)}, u32[]{:S(2)}, u32[]{:S(2)}) %collective-permute-start.14) | collective-permute-done | bytes 262176 | tf_op jit(solution)/shard_map/ppermute | solution.py:176
  63.8 0.5 collective-permute-start.15
  64.3 1.8 %collective-permute-done.24.x_ref = f32[64,1024]{1,0:T(8,128)S(1)} collective-permute-done((f32[64,1024]{1,0:T(8,128)S(1)}, f32[64,1024]{1,0:T(8,128)S(1)}, u32[]{:S(2)}, u32[]{:S(2)}) %collective-permute-start.24) | collective-permute-done | bytes 262176 | tf_op jit(solution)/shard_map/ppermute | solution.py:196
  66.1 2.4 %collective-permute-start.22 = (f32[64,1024]{1,0:T(8,128)S(1)}, f32[64,1024]{1,0:T(8,128)S(1)}, u32[]{:S(2)}, u32[]{:S(2)}) collective-permute-start(f32[64,1024]{1,0:T(8,128)S(1)} %shard_map.56.refs_20_.refs_4_), channel_id=1, source_target_pairs={{0,2},{1,3},{2,0},{3,1},{4,6},{5,7},{6,4},{7,5},{8,10},{9,11},{10,... | collective-permute-start | bytes 786440 | tf_op jit(solution)/shard_map/ppermute | solution.py:176
  68.6 0.8 shard_map.57.refs_24_.refs_8_
  70.1 5.6 %collective-permute-done.22.refs_22_.refs_6_ = f32[64,1024]{1,0:T(8,128)S(1)} collective-permute-done((f32[64,1024]{1,0:T(8,128)S(1)}, f32[64,1024]{1,0:T(8,128)S(1)}, u32[]{:S(2)}, u32[]{:S(2)}) %collective-permute-start.22) | collective-permute-done | bytes 262176 | tf_op jit(solution)/shard_map/ppermute | solution.py:176
  75.7 4.8 %collective-permute-done.26.refs_26_.refs_10_ = f32[64,1024]{1,0:T(8,128)S(1)} collective-permute-done((f32[64,1024]{1,0:T(8,128)S(1)}, f32[64,1024]{1,0:T(8,128)S(1)}, u32[]{:S(2)}, u32[]{:S(2)}) %collective-permute-start.26) | collective-permute-done | bytes 262176 | tf_op jit(solution)/shard_map/ppermute | solution.py:176
  80.6 1.8 %shard_map.59 = (f32[64,512]{1,0:T(8,128)S(1)}, f32[64,512]{1,0:T(8,128)S(1)}, f32[64,512]{1,0:T(8,128)S(1)}, f32[64,512]{1,0:T(8,128)S(1)}, f32[64,512]{1,0:T(8...) custom-call(f32[1,1024]{1,0:T(1,128)S(1)} %copy-done.2, ...), custom_call_target="tpu_custom_call" | custom-call | flops 1610612736 | bytes 7344128 | tf_op jit(solution)/shard_map/pallas_call | solution.py:25
  82.3 2.0 %collective-permute-start.28 = (f32[64,512]{1,0:T(8,128)S(1)}, f32[64,512]{1,0:T(8,128)S(1)}, u32[]{:S(2)}, u32[]{:S(2)}) collective-permute-start(f32[64,512]{1,0:T(8,128)S(1)} %get-tuple-element.19), channel_id=1, source_target_pairs={{0,4},{4,0},{8,12},{12,8},{16,20},{20,16},{24,28},{28,24},{1,5},{5... | collective-permute-start | bytes 393224 | tf_op jit(solution)/shard_map/ppermute | solution.py:176
  84.3 1.1 collective-permute-start.29
  85.3 0.5 collective-permute-start.30
  85.9 6.3 %collective-permute-start.31 = (f32[64,512]{1,0:T(8,128)S(1)}, f32[64,512]{1,0:T(8,128)S(1)}, u32[]{:S(2)}, u32[]{:S(2)}) collective-permute-start(f32[64,512]{1,0:T(8,128)S(1)} %get-tuple-element.22), channel_id=1, source_target_pairs={{0,16},{4,20},{8,24},{12,28},{16,0},{20,4},{24,8},{28,12},{1,17},{... | collective-permute-start | bytes 393224 | tf_op jit(solution)/shard_map/ppermute | solution.py:176
  92.2 0.8 shard_map.60
  93.0 2.6 %collective-permute-start.33 = (f32[64,512]{1,0:T(8,128)S(1)}, f32[64,512]{1,0:T(8,128)S(1)}, u32[]{:S(2)}, u32[]{:S(2)}) collective-permute-start(f32[64,512]{1,0:T(8,128)S(1)} %get-tuple-element.24), channel_id=1, source_target_pairs={{0,24},{4,28},{8,16},{12,20},{16,8},{20,12},{24,0},{28,4},{1,25},{... | collective-permute-start | bytes 393224 | tf_op jit(solution)/shard_map/ppermute | solution.py:176
  95.6 2.2 %collective-permute-start.34 = (f32[64,512]{1,0:T(8,128)S(1)}, f32[64,512]{1,0:T(8,128)S(1)}, u32[]{:S(2)}, u32[]{:S(2)}) collective-permute-start(f32[64,512]{1,0:T(8,128)S(1)} %get-tuple-element.25), channel_id=1, source_target_pairs={{0,28},{4,24},{8,20},{12,16},{16,12},{20,8},{24,4},{28,0},{1,29},{... | collective-permute-start | bytes 393224 | tf_op jit(solution)/shard_map/ppermute | solution.py:176
  97.8 1.3 %collective-permute-start.35 = (f32[64,512]{1,0:T(8,128)S(1)}, f32[64,512]{1,0:T(8,128)S(1)}, u32[]{:S(2)}, u32[]{:S(2)}) collective-permute-start(f32[64,512]{1,0:T(8,128)S(1)} %get-tuple-element.26), channel_id=1, source_target_pairs={{28,0},{24,16},{29,4},{25,20},{30,8},{26,24},{31,12},{27,28}} | collective-permute-start | bytes 393224 | tf_op jit(solution)/shard_map/ppermute | solution.py:247
  99.1 1.3 %collective-permute-start.36 = (f32[64,512]{1,0:T(8,128)S(1)}, f32[64,512]{1,0:T(8,128)S(1)}, u32[]{:S(2)}, u32[]{:S(2)}) collective-permute-start(f32[64,512]{1,0:T(8,128)S(1)} %get-tuple-element.27), channel_id=1, source_target_pairs={{28,16},{24,0},{29,20},{25,4},{30,24},{26,8},{31,28},{27,12}} | collective-permute-start | bytes 393224 | tf_op jit(solution)/shard_map/ppermute | solution.py:247
  100.4 2.2 %shard_map.58 = f32[1024,512]{1,0:T(8,128)} custom-call(f32[256,1024]{1,0:T(8,128)S(1)} %get-tuple-element.15.start_ref, f32[64,1024]{1,0:T(8,128)S(1)} %shard_map.51.refs_0_, f32[64,1024]{1,0:T(8,128)S(1)} %collective-permute-done.1.refs_1_, f32[64,1024]{1,0:T(8,128)S(1)} %collective-permute-done.2.refs_2_, f32[64,1024]{1,0:T(8,128)S(1)} %collective-permute-done.3.refs_3_, ...), custom_call_target="tpu_custom_call" | custom-call | bytes 10485760 | tf_op jit(solution)/shard_map/pallas_call | solution.py:25
  102.6 11.5 %collective-permute-done.32 = f32[64,512]{1,0:T(8,128)S(1)} collective-permute-done((f32[64,512]{1,0:T(8,128)S(1)}, f32[64,512]{1,0:T(8,128)S(1)}, u32[]{:S(2)}, u32[]{:S(2)}) %collective-permute-start.32) | collective-permute-done | bytes 131104 | tf_op jit(solution)/shard_map/ppermute | solution.py:176
  114.2 1.4 %collective-permute-done.36 = f32[64,512]{1,0:T(8,128)S(1)} collective-permute-done((f32[64,512]{1,0:T(8,128)S(1)}, f32[64,512]{1,0:T(8,128)S(1)}, u32[]{:S(2)}, u32[]{:S(2)}) %collective-permute-start.36) | collective-permute-done | bytes 131104 | tf_op jit(solution)/shard_map/ppermute | solution.py:247
  115.6 0.8 add_bitcast_fusion
  (46 shorter events, 1.5 us)
Async XLA Ops:
  0.6 4.6 %copy-start.1 = (f32[1,1024,256]{2,1,0:T(8,128)S(1)}, f32[1,1024,256]{2,1,0:T(8,128)}, u32[]{:S(2)}) copy-start(f32[1,1024,256]{2,1,0:T(8,128)} %param.4) | copy-start | bytes 3145732
  2.2 12.4 %collective-permute-start = (f32[64,1024]{1,0:T(8,128)S(1)}, f32[64,1024]{1,0:T(8,128)S(1)}, u32[]{:S(2)}, u32[]{:S(2)}) collective-permute-start(f32[64,1024]{1,0:T(8,128)S(1)} %bitcast.11), channel_id=1, source_target_pairs={{0,4},{4,8},{8,12},{12,16},{16,20},{20,24},{24,28},{28,0},{1,5},{5... | collective-permute-start | bytes 786440 | tf_op jit(solution)/shard_map/ppermute | solution.py:196
  5.2 2.2 %copy-start = (f32[1,1024,1024]{2,1,0:T(8,128)S(1)}, f32[1,1024,1024]{2,1,0:T(8,128)}, u32[]{:S(2)}) copy-start(f32[1,1024,1024]{2,1,0:T(8,128)} %param.3) | copy-start | bytes 12582916
  15.4 0.7 collective-permute-start.4
  16.8 13.7 %collective-permute-start.8 = (f32[64,1024]{1,0:T(8,128)S(1)}, f32[64,1024]{1,0:T(8,128)S(1)}, u32[]{:S(2)}, u32[]{:S(2)}) collective-permute-start(f32[64,1024]{1,0:T(8,128)S(1)} %shard_map.52.refs_4_), channel_id=1, source_target_pairs={{8,12},{12,16},{16,20},{20,24},{24,28},{28,8},{0,4},{4,0},{9,13},{... | collective-permute-start | bytes 786440 | tf_op jit(solution)/shard_map/ppermute | solution.py:196
  31.3 8.4 %collective-permute-start.12 = (f32[64,1024]{1,0:T(8,128)S(1)}, f32[64,1024]{1,0:T(8,128)S(1)}, u32[]{:S(2)}, u32[]{:S(2)}) collective-permute-start(f32[64,1024]{1,0:T(8,128)S(1)} %shard_map.53.refs_8_), channel_id=1, source_target_pairs={{12,16},{16,20},{20,24},{24,28},{28,12},{0,4},{4,0},{8,8},{13,17},... | collective-permute-start | bytes 786440 | tf_op jit(solution)/shard_map/ppermute | solution.py:196
  34.9 9.3 %collective-permute-start.2 = (f32[64,1024]{1,0:T(8,128)S(1)}, f32[64,1024]{1,0:T(8,128)S(1)}, u32[]{:S(2)}, u32[]{:S(2)}) collective-permute-start(f32[64,1024]{1,0:T(8,128)S(1)} %shard_map.51.refs_0_), channel_id=1, source_target_pairs={{0,2},{1,3},{2,0},{3,1},{4,6},{5,7},{6,4},{7,5},{8,10},{9,11},{10,... | collective-permute-start | bytes 786440 | tf_op jit(solution)/shard_map/ppermute | solution.py:176
  40.5 6.4 %collective-permute-start.16 = (f32[64,1024]{1,0:T(8,128)S(1)}, f32[64,1024]{1,0:T(8,128)S(1)}, u32[]{:S(2)}, u32[]{:S(2)}) collective-permute-start(f32[64,1024]{1,0:T(8,128)S(1)} %shard_map.54.refs_12_), channel_id=1, source_target_pairs={{16,20},{20,24},{24,28},{28,16},{0,4},{4,0},{8,12},{12,8},{17,21},... | collective-permute-start | bytes 786440 | tf_op jit(solution)/shard_map/ppermute | solution.py:196
  42.5 9.1 %collective-permute-start.1 = (f32[64,1024]{1,0:T(8,128)S(1)}, f32[64,1024]{1,0:T(8,128)S(1)}, u32[]{:S(2)}, u32[]{:S(2)}) collective-permute-start(f32[64,1024]{1,0:T(8,128)S(1)} %shard_map.51.refs_0_), channel_id=1, source_target_pairs={{0,1},{1,0},{2,3},{3,2},{4,5},{5,4},{6,7},{7,6},{8,9},{9,8},{10,11... | collective-permute-start | bytes 786440 | tf_op jit(solution)/shard_map/ppermute | solution.py:176
  42.5 10.7 %collective-permute-start.6 = (f32[64,1024]{1,0:T(8,128)S(1)}, f32[64,1024]{1,0:T(8,128)S(1)}, u32[]{:S(2)}, u32[]{:S(2)}) collective-permute-start(f32[64,1024]{1,0:T(8,128)S(1)} %shard_map.52.refs_4_), channel_id=1, source_target_pairs={{0,2},{1,3},{2,0},{3,1},{4,6},{5,7},{6,4},{7,5},{8,10},{9,11},{10,... | collective-permute-start | bytes 786440 | tf_op jit(solution)/shard_map/ppermute | solution.py:176
  44.0 9.2 %collective-permute-start.5 = (f32[64,1024]{1,0:T(8,128)S(1)}, f32[64,1024]{1,0:T(8,128)S(1)}, u32[]{:S(2)}, u32[]{:S(2)}) collective-permute-start(f32[64,1024]{1,0:T(8,128)S(1)} %shard_map.52.refs_4_), channel_id=1, source_target_pairs={{0,1},{1,0},{2,3},{3,2},{4,5},{5,4},{6,7},{7,6},{8,9},{9,8},{10,11... | collective-permute-start | bytes 786440 | tf_op jit(solution)/shard_map/ppermute | solution.py:176
  44.3 9.4 %collective-permute-start.3 = (f32[64,1024]{1,0:T(8,128)S(1)}, f32[64,1024]{1,0:T(8,128)S(1)}, u32[]{:S(2)}, u32[]{:S(2)}) collective-permute-start(f32[64,1024]{1,0:T(8,128)S(1)} %collective-permute-done.2.refs_2_), channel_id=1, source_target_pairs={{0,1},{1,0},{2,3},{3,2},{4,5},{5,4},{6,7},{7,6},{8,9},{9,8},{10,11... | collective-permute-start | bytes 786440 | tf_op jit(solution)/shard_map/ppermute | solution.py:176
  47.7 8.3 %collective-permute-start.20 = (f32[64,1024]{1,0:T(8,128)S(1)}, f32[64,1024]{1,0:T(8,128)S(1)}, u32[]{:S(2)}, u32[]{:S(2)}) collective-permute-start(f32[64,1024]{1,0:T(8,128)S(1)} %shard_map.55.refs_16_.refs_0_), channel_id=1, source_target_pairs={{20,24},{24,28},{28,20},{0,4},{4,0},{8,12},{12,8},{16,16},{21,25},... | collective-permute-start | bytes 786440 | tf_op jit(solution)/shard_map/ppermute | solution.py:196
  51.6 8.1 %collective-permute-start.10 = (f32[64,1024]{1,0:T(8,128)S(1)}, f32[64,1024]{1,0:T(8,128)S(1)}, u32[]{:S(2)}, u32[]{:S(2)}) collective-permute-start(f32[64,1024]{1,0:T(8,128)S(1)} %shard_map.53.refs_8_), channel_id=1, source_target_pairs={{0,2},{1,3},{2,0},{3,1},{4,6},{5,7},{6,4},{7,5},{8,10},{9,11},{10,... | collective-permute-start | bytes 786440 | tf_op jit(solution)/shard_map/ppermute | solution.py:176
  53.2 6.6 %collective-permute-start.9 = (f32[64,1024]{1,0:T(8,128)S(1)}, f32[64,1024]{1,0:T(8,128)S(1)}, u32[]{:S(2)}, u32[]{:S(2)}) collective-permute-start(f32[64,1024]{1,0:T(8,128)S(1)} %shard_map.53.refs_8_), channel_id=1, source_target_pairs={{0,1},{1,0},{2,3},{3,2},{4,5},{5,4},{6,7},{7,6},{8,9},{9,8},{10,11... | collective-permute-start | bytes 786440 | tf_op jit(solution)/shard_map/ppermute | solution.py:176
  53.2 6.6 %collective-permute-start.7 = (f32[64,1024]{1,0:T(8,128)S(1)}, f32[64,1024]{1,0:T(8,128)S(1)}, u32[]{:S(2)}, u32[]{:S(2)}) collective-permute-start(f32[64,1024]{1,0:T(8,128)S(1)} %collective-permute-done.6.refs_6_), channel_id=1, source_target_pairs={{0,1},{1,0},{2,3},{3,2},{4,5},{5,4},{6,7},{7,6},{8,9},{9,8},{10,11... | collective-permute-start | bytes 786440 | tf_op jit(solution)/shard_map/ppermute | solution.py:176
  53.7 10.1 %collective-permute-start.14 = (f32[64,1024]{1,0:T(8,128)S(1)}, f32[64,1024]{1,0:T(8,128)S(1)}, u32[]{:S(2)}, u32[]{:S(2)}) collective-permute-start(f32[64,1024]{1,0:T(8,128)S(1)} %shard_map.54.refs_12_), channel_id=1, source_target_pairs={{0,2},{1,3},{2,0},{3,1},{4,6},{5,7},{6,4},{7,5},{8,10},{9,11},{10,... | collective-permute-start | bytes 786440 | tf_op jit(solution)/shard_map/ppermute | solution.py:176
  56.0 7.8 %collective-permute-start.13 = (f32[64,1024]{1,0:T(8,128)S(1)}, f32[64,1024]{1,0:T(8,128)S(1)}, u32[]{:S(2)}, u32[]{:S(2)}) collective-permute-start(f32[64,1024]{1,0:T(8,128)S(1)} %shard_map.54.refs_12_), channel_id=1, source_target_pairs={{0,1},{1,0},{2,3},{3,2},{4,5},{5,4},{6,7},{7,6},{8,9},{9,8},{10,11... | collective-permute-start | bytes 786440 | tf_op jit(solution)/shard_map/ppermute | solution.py:176
  56.8 23.8 %copy-start.2 = (f32[1,1024]{1,0:T(1,128)S(1)}, f32[1,1024]{1,0:T(1,128)}, u32[]{:S(2)}) copy-start(f32[1,1024]{1,0:T(1,128)} %weight_ref.3) | copy-start | bytes 12292
  59.8 6.4 %collective-permute-start.24 = (f32[64,1024]{1,0:T(8,128)S(1)}, f32[64,1024]{1,0:T(8,128)S(1)}, u32[]{:S(2)}, u32[]{:S(2)}) collective-permute-start(f32[64,1024]{1,0:T(8,128)S(1)} %shard_map.56.refs_20_.refs_4_), channel_id=1, source_target_pairs={{24,28},{28,24},{0,4},{4,0},{8,12},{12,8},{16,20},{20,16},{25,29},... | collective-permute-start | bytes 786440 | tf_op jit(solution)/shard_map/ppermute | solution.py:196
  59.8 9.6 %collective-permute-start.11 = (f32[64,1024]{1,0:T(8,128)S(1)}, f32[64,1024]{1,0:T(8,128)S(1)}, u32[]{:S(2)}, u32[]{:S(2)}) collective-permute-start(f32[64,1024]{1,0:T(8,128)S(1)} %collective-permute-done.10.refs_10_), channel_id=1, source_target_pairs={{0,1},{1,0},{2,3},{3,2},{4,5},{5,4},{6,7},{7,6},{8,9},{9,8},{10,11... | collective-permute-start | bytes 786440 | tf_op jit(solution)/shard_map/ppermute | solution.py:176
  59.8 9.7 %collective-permute-start.18 = (f32[64,1024]{1,0:T(8,128)S(1)}, f32[64,1024]{1,0:T(8,128)S(1)}, u32[]{:S(2)}, u32[]{:S(2)}) collective-permute-start(f32[64,1024]{1,0:T(8,128)S(1)} %shard_map.55.refs_16_.refs_0_), channel_id=1, source_target_pairs={{0,2},{1,3},{2,0},{3,1},{4,6},{5,7},{6,4},{7,5},{8,10},{9,11},{10,... | collective-permute-start | bytes 786440 | tf_op jit(solution)/shard_map/ppermute | solution.py:176
  63.8 5.8 %collective-permute-start.17 = (f32[64,1024]{1,0:T(8,128)S(1)}, f32[64,1024]{1,0:T(8,128)S(1)}, u32[]{:S(2)}, u32[]{:S(2)}) collective-permute-start(f32[64,1024]{1,0:T(8,128)S(1)} %shard_map.55.refs_16_.refs_0_), channel_id=1, source_target_pairs={{0,1},{1,0},{2,3},{3,2},{4,5},{5,4},{6,7},{7,6},{8,9},{9,8},{10,11... | collective-permute-start | bytes 786440 | tf_op jit(solution)/shard_map/ppermute | solution.py:176
  63.8 6.3 %collective-permute-start.15 = (f32[64,1024]{1,0:T(8,128)S(1)}, f32[64,1024]{1,0:T(8,128)S(1)}, u32[]{:S(2)}, u32[]{:S(2)}) collective-permute-start(f32[64,1024]{1,0:T(8,128)S(1)} %collective-permute-done.14.refs_14_), channel_id=1, source_target_pairs={{0,1},{1,0},{2,3},{3,2},{4,5},{5,4},{6,7},{7,6},{8,9},{9,8},{10,11... | collective-permute-start | bytes 786440 | tf_op jit(solution)/shard_map/ppermute | solution.py:176
  66.1 9.6 %collective-permute-start.22 = (f32[64,1024]{1,0:T(8,128)S(1)}, f32[64,1024]{1,0:T(8,128)S(1)}, u32[]{:S(2)}, u32[]{:S(2)}) collective-permute-start(f32[64,1024]{1,0:T(8,128)S(1)} %shard_map.56.refs_20_.refs_4_), channel_id=1, source_target_pairs={{0,2},{1,3},{2,0},{3,1},{4,6},{5,7},{6,4},{7,5},{8,10},{9,11},{10,... | collective-permute-start | bytes 786440 | tf_op jit(solution)/shard_map/ppermute | solution.py:176
  69.4 11.2 %collective-permute-start.26 = (f32[64,1024]{1,0:T(8,128)S(1)}, f32[64,1024]{1,0:T(8,128)S(1)}, u32[]{:S(2)}, u32[]{:S(2)}) collective-permute-start(f32[64,1024]{1,0:T(8,128)S(1)} %shard_map.57.refs_24_.refs_8_), channel_id=1, source_target_pairs={{0,2},{1,3},{2,0},{3,1},{4,6},{5,7},{6,4},{7,5},{8,10},{9,11},{10,... | collective-permute-start | bytes 786440 | tf_op jit(solution)/shard_map/ppermute | solution.py:176
  69.5 11.1 %collective-permute-start.19 = (f32[64,1024]{1,0:T(8,128)S(1)}, f32[64,1024]{1,0:T(8,128)S(1)}, u32[]{:S(2)}, u32[]{:S(2)}) collective-permute-start(f32[64,1024]{1,0:T(8,128)S(1)} %collective-permute-done.18.refs_18_.refs_2_), channel_id=1, source_target_pairs={{0,1},{1,0},{2,3},{3,2},{4,5},{5,4},{6,7},{7,6},{8,9},{9,8},{10,11... | collective-permute-start | bytes 786440 | tf_op jit(solution)/shard_map/ppermute | solution.py:176
  69.6 14.7 %collective-permute-start.21 = (f32[64,1024]{1,0:T(8,128)S(1)}, f32[64,1024]{1,0:T(8,128)S(1)}, u32[]{:S(2)}, u32[]{:S(2)}) collective-permute-start(f32[64,1024]{1,0:T(8,128)S(1)} %shard_map.56.refs_20_.refs_4_), channel_id=1, source_target_pairs={{0,1},{1,0},{2,3},{3,2},{4,5},{5,4},{6,7},{7,6},{8,9},{9,8},{10,11... | collective-permute-start | bytes 786440 | tf_op jit(solution)/shard_map/ppermute | solution.py:176
  70.1 15.3 %collective-permute-start.25 = (f32[64,1024]{1,0:T(8,128)S(1)}, f32[64,1024]{1,0:T(8,128)S(1)}, u32[]{:S(2)}, u32[]{:S(2)}) collective-permute-start(f32[64,1024]{1,0:T(8,128)S(1)} %shard_map.57.refs_24_.refs_8_), channel_id=1, source_target_pairs={{0,1},{1,0},{2,3},{3,2},{4,5},{5,4},{6,7},{7,6},{8,9},{9,8},{10,11... | collective-permute-start | bytes 786440 | tf_op jit(solution)/shard_map/ppermute | solution.py:176
  75.7 10.1 %collective-permute-start.23 = (f32[64,1024]{1,0:T(8,128)S(1)}, f32[64,1024]{1,0:T(8,128)S(1)}, u32[]{:S(2)}, u32[]{:S(2)}) collective-permute-start(f32[64,1024]{1,0:T(8,128)S(1)} %collective-permute-done.22.refs_22_.refs_6_), channel_id=1, source_target_pairs={{0,1},{1,0},{2,3},{3,2},{4,5},{5,4},{6,7},{7,6},{8,9},{9,8},{10,11... | collective-permute-start | bytes 786440 | tf_op jit(solution)/shard_map/ppermute | solution.py:176
  80.5 11.6 %collective-permute-start.27 = (f32[64,1024]{1,0:T(8,128)S(1)}, f32[64,1024]{1,0:T(8,128)S(1)}, u32[]{:S(2)}, u32[]{:S(2)}) collective-permute-start(f32[64,1024]{1,0:T(8,128)S(1)} %collective-permute-done.26.refs_26_.refs_10_), channel_id=1, source_target_pairs={{0,1},{1,0},{2,3},{3,2},{4,5},{5,4},{6,7},{7,6},{8,9},{9,8},{10,11... | collective-permute-start | bytes 786440 | tf_op jit(solution)/shard_map/ppermute | solution.py:176
  82.3 10.7 %collective-permute-start.28 = (f32[64,512]{1,0:T(8,128)S(1)}, f32[64,512]{1,0:T(8,128)S(1)}, u32[]{:S(2)}, u32[]{:S(2)}) collective-permute-start(f32[64,512]{1,0:T(8,128)S(1)} %get-tuple-element.19), channel_id=1, source_target_pairs={{0,4},{4,0},{8,12},{12,8},{16,20},{20,16},{24,28},{28,24},{1,5},{5... | collective-permute-start | bytes 393224 | tf_op jit(solution)/shard_map/ppermute | solution.py:176
  84.3 11.3 %collective-permute-start.29 = (f32[64,512]{1,0:T(8,128)S(1)}, f32[64,512]{1,0:T(8,128)S(1)}, u32[]{:S(2)}, u32[]{:S(2)}) collective-permute-start(f32[64,512]{1,0:T(8,128)S(1)} %get-tuple-element.20), channel_id=1, source_target_pairs={{0,8},{4,12},{8,0},{12,4},{16,24},{20,28},{24,16},{28,20},{1,9},{5... | collective-permute-start | bytes 393224 | tf_op jit(solution)/shard_map/ppermute | solution.py:176
  85.3 12.5 %collective-permute-start.30 = (f32[64,512]{1,0:T(8,128)S(1)}, f32[64,512]{1,0:T(8,128)S(1)}, u32[]{:S(2)}, u32[]{:S(2)}) collective-permute-start(f32[64,512]{1,0:T(8,128)S(1)} %get-tuple-element.21), channel_id=1, source_target_pairs={{0,12},{4,8},{8,4},{12,0},{16,28},{20,24},{24,20},{28,16},{1,13},{... | collective-permute-start | bytes 393224 | tf_op jit(solution)/shard_map/ppermute | solution.py:176
  85.9 13.2 %collective-permute-start.31 = (f32[64,512]{1,0:T(8,128)S(1)}, f32[64,512]{1,0:T(8,128)S(1)}, u32[]{:S(2)}, u32[]{:S(2)}) collective-permute-start(f32[64,512]{1,0:T(8,128)S(1)} %get-tuple-element.22), channel_id=1, source_target_pairs={{0,16},{4,20},{8,24},{12,28},{16,0},{20,4},{24,8},{28,12},{1,17},{... | collective-permute-start | bytes 393224 | tf_op jit(solution)/shard_map/ppermute | solution.py:176
  92.1 22.0 %collective-permute-start.32 = (f32[64,512]{1,0:T(8,128)S(1)}, f32[64,512]{1,0:T(8,128)S(1)}, u32[]{:S(2)}, u32[]{:S(2)}) collective-permute-start(f32[64,512]{1,0:T(8,128)S(1)} %get-tuple-element.23), channel_id=1, source_target_pairs={{0,20},{4,16},{8,28},{12,24},{16,4},{20,0},{24,12},{28,8},{1,21},{... | collective-permute-start | bytes 393224 | tf_op jit(solution)/shard_map/ppermute | solution.py:176
  93.0 21.1 %collective-permute-start.33 = (f32[64,512]{1,0:T(8,128)S(1)}, f32[64,512]{1,0:T(8,128)S(1)}, u32[]{:S(2)}, u32[]{:S(2)}) collective-permute-start(f32[64,512]{1,0:T(8,128)S(1)} %get-tuple-element.24), channel_id=1, source_target_pairs={{0,24},{4,28},{8,16},{12,20},{16,8},{20,12},{24,0},{28,4},{1,25},{... | collective-permute-start | bytes 393224 | tf_op jit(solution)/shard_map/ppermute | solution.py:176
  95.6 18.6 %collective-permute-start.34 = (f32[64,512]{1,0:T(8,128)S(1)}, f32[64,512]{1,0:T(8,128)S(1)}, u32[]{:S(2)}, u32[]{:S(2)}) collective-permute-start(f32[64,512]{1,0:T(8,128)S(1)} %get-tuple-element.25), channel_id=1, source_target_pairs={{0,28},{4,24},{8,20},{12,16},{16,12},{20,8},{24,4},{28,0},{1,29},{... | collective-permute-start | bytes 393224 | tf_op jit(solution)/shard_map/ppermute | solution.py:176
  97.8 16.4 %collective-permute-start.35 = (f32[64,512]{1,0:T(8,128)S(1)}, f32[64,512]{1,0:T(8,128)S(1)}, u32[]{:S(2)}, u32[]{:S(2)}) collective-permute-start(f32[64,512]{1,0:T(8,128)S(1)} %get-tuple-element.26), channel_id=1, source_target_pairs={{28,0},{24,16},{29,4},{25,20},{30,8},{26,24},{31,12},{27,28}} | collective-permute-start | bytes 393224 | tf_op jit(solution)/shard_map/ppermute | solution.py:247
  99.1 16.5 %collective-permute-start.36 = (f32[64,512]{1,0:T(8,128)S(1)}, f32[64,512]{1,0:T(8,128)S(1)}, u32[]{:S(2)}, u32[]{:S(2)}) collective-permute-start(f32[64,512]{1,0:T(8,128)S(1)} %get-tuple-element.27), channel_id=1, source_target_pairs={{28,16},{24,0},{29,20},{25,4},{30,24},{26,8},{31,28},{27,12}} | collective-permute-start | bytes 393224 | tf_op jit(solution)/shard_map/ppermute | solution.py:247
where the time goes:
time: 117 us; the launch traced here: 116 us
  starting transfers between devices  51.9 us (44%)
  waiting for transfers between devices  47.2 us (40%)
  Pallas kernels  11.9 us (10%)
  local copies, waits for them, and re-layouts  3.71 us (3%)
    ppermute x28, starting transfers between devices, xor_swap(): return lax.ppermute(value, axis, [(i, i ^ by) for i in range(devices)])  26.9 us
    ppermute x28, waiting for transfers between devices, xor_swap(): return lax.ppermute(value, axis, [(i, i ^ by) for i in range(devices)])  26.5 us
    ppermute x7, starting transfers between devices, local(): moved = lax.ppermute(newest, 'seg', wave_pairs(nseg, tick))  22.4 us
    ppermute x7, waiting for transfers between devices, local(): moved = lax.ppermute(newest, 'seg', wave_pairs(nseg, tick))  19.3 us
    pallas_call x11, Pallas kernels, call(): pl.pallas_call(kernel, out_shape=outs, in_specs=[VMEM] * len(args), out_s...  11.9 us
    ppermute x2, starting transfers between devices, local(): terms.append(lax.ppermute(late[2 * i + half], ('seg', 'ctl'), pairs))  2.57 us
  transfers between devices with their start and end apart: 37, of which 12 were waited for; matrix products, arithmetic and copies ran while one was open for 0% of the time, Pallas kernels for 8%

commit v1 on v0

--- a/solution.py
+++ b/solution.py
@@ -110,8 +110,8 @@
 
 def early_kernel(layout, weight_ref, start_ref, *refs):
     nseg, pieces = layout.nseg, len(layout.ticks) * layout.nctl
-    piece_refs, out_refs = refs[:pieces], refs[pieces : pieces + nseg]
-    sens, high, low, w_high, w_low, tile = refs[pieces + nseg :]
+    piece_refs, out_refs = refs[:pieces], refs[pieces:-6]
+    sens, high, low, w_high, w_low, tile = refs[-6:]
     layout.gather(sens, lax.axis_index("ctl"), start_ref, piece_refs, nseg - 2)
     for i in range(0, sens.shape[0], 128):
         at = slice(i, i + 128)
@@ -125,8 +125,13 @@
             tile[nu + k : nu + k + 128, i : i + 128] = tile[i : i + 128, nu + k : nu + k + 128].T
     seg = lax.axis_index("seg")
     rows = tile.shape[0] // nseg
-    for r in range(nseg):
-        out_refs[r][...] = tile[pl.ds(pl.multiple_of((seg ^ r) * rows, rows), rows), :]
+    for r, out_ref in enumerate(out_refs):
+        out_ref[...] = tile[pl.ds(pl.multiple_of((seg ^ r) * rows, rows), rows), :]
+
+
+def merge_kernel(*refs):
+    *term_refs, sum_ref = refs
+    sum_ref[...] = sum(ref[...] for ref in term_refs)
 
 
 def late_kernel(layout, weight_ref, *refs):
@@ -213,23 +218,32 @@
     tall = (2 * nu, nx)
     body, given = kernel_of(early_kernel, list(range(1, nseg - 2)))
     early = call(
-            body,
+        body,
         [out((rows, 2 * nu))] * nseg,
         weights,
         start,
         *given,
-        scratch=[pltpu.VMEM(tall, F32)] + [pltpu.VMEM(tall, BF16)] * 4 + [pltpu.VMEM((2 * nu, 2 * nu), F32)],
+        scratch=[pltpu.VMEM(tall, F32)]
+        + [pltpu.VMEM(tall, BF16)] * 4
+        + [pltpu.VMEM((2 * nu, 2 * nu), F32)],
         flops=6 * nx * (2 * nu) ** 2,
     )
+    half = nseg // 2
+    terms = {}
+    for r in range(1, half):
+        for base in (half, 0):
+            terms[base + r] = xor_swap(early[base + r], "seg", r)
+    (far,) = call(
+        merge_kernel, [out((rows, 2 * nu))], early[half], *[terms[half + r] for r in range(1, half)]
+    )
+    far = xor_swap(far, "seg", half)
     total = early[0]
-    terms = []
-    for r in range(1, nseg):
-        terms.append(xor_swap(early[r], "seg", r))
+    terms = [terms[r] for r in range(1, half)] + [far]
 
     late_ticks = sorted({nseg - 1 - stride, nseg - 2 - stride, nseg - 2, nseg - 1})
     body, given = kernel_of(late_kernel, late_ticks)
     late = call(
-            body,
+        body,
         [out((rows, 2 * nu))] * (2 * stride),
         weights,
         *given,

time: 117 us -> 122 us (1.043)
  waiting for transfers between devices: 47.2 us -> 58.5 us
  starting transfers between devices: 51.9 us -> 46 us
    ppermute x2, waiting for transfers between devices: 1.41 us -> 8.1 us  [local(): terms.append(lax.ppermute(late[2 * i + half], ('seg', 'ctl'), pairs))]
    ppermute x28, starting transfers between devices: 26.9 us -> 20.4 us  [xor_swap(): return lax.ppermute(value, axis, [(i, i ^ by) for i in range(devices)])]
    ppermute x28, waiting for transfers between devices: 26.5 us -> 30.5 us  [xor_swap(): return lax.ppermute(value, axis, [(i, i ^ by) for i in range(devices)])]
    pallas_call x11 -> x12, Pallas kernels: 11.9 us -> 12.1 us  [call(): pl.pallas_call(kernel, out_shape=outs, in_specs=[VMEM] * len(args), out_s...]
  transfers between devices with their start and end apart: 37 -> 37, of which waited for: 12 -> 14; matrix products, arithmetic and copies ran while one was open for 0% -> 0% of each run, Pallas kernels for 8% -> 7%
where the time goes in v1:
time: 122 us
  waiting for transfers between devices  58.5 us (48%)
  starting transfers between devices  46 us (38%)
  Pallas kernels  12.1 us (10%)
  local copies, waits for them, and re-layouts  3.71 us (3%)
    ppermute x28, waiting for transfers between devices, xor_swap(): return lax.ppermute(value, axis, [(i, i ^ by) for i in range(devices)])  30.5 us
    ppermute x7, starting transfers between devices, local(): moved = lax.ppermute(newest, 'seg', wave_pairs(nseg, tick))  23 us
    ppermute x28, starting transfers between devices, xor_swap(): return lax.ppermute(value, axis, [(i, i ^ by) for i in range(devices)])  20.4 us
    ppermute x7, waiting for transfers between devices, local(): moved = lax.ppermute(newest, 'seg', wave_pairs(nseg, tick))  20 us
    pallas_call x12, Pallas kernels, call(): pl.pallas_call(kernel, out_shape=outs, in_specs=[VMEM] * len(args), out_s...  12.1 us
    ppermute x2, waiting for transfers between devices, local(): terms.append(lax.ppermute(late[2 * i + half], ('seg', 'ctl'), pairs))  8.1 us
    ppermute x2, starting transfers between devices, local(): terms.append(lax.ppermute(late[2 * i + half], ('seg', 'ctl'), pairs))  2.58 us
  transfers between devices with their start and end apart: 37, of which 14 were waited for; matrix products, arithmetic and copies ran while one was open for 0% of the time, Pallas kernels for 7%

profile of v1, /device:TPU:0, one launch (start us, length us, event | category | flops | bytes accessed | tf_op | source)
XLA Modules:
  0.0 121.9 jit_solution(6927557105930614804)
XLA Ops:
  0.6 1.3 %constant_dynamic-slice_fusion = f32[1,1024,64]{2,1,0:T(8,128)S(1)} fusion(f32[1,1024,256]{2,1,0:T(8,128)} %param.4, s32[]{:T(128)S(6)} %select_n.3), kind=kLoop, calls=%fused_computation.1 | loop fusion | bytes 524292 | tf_op jit(solution)/shard_map/dynamic_slice | solution.py:193
  2.2 3.0 %collective-permute-start = (f32[64,1024]{1,0:T(8,128)S(1)}, f32[64,1024]{1,0:T(8,128)S(1)}, u32[]{:S(2)}, u32[]{:S(2)}) collective-permute-start(f32[64,1024]{1,0:T(8,128)S(1)} %bitcast.11), channel_id=1, source_target_pairs={{0,4},{4,8},{8,12},{12,16},{16,20},{20,24},{24,28},{28,0},{1,5},{5... | collective-permute-start | bytes 786440 | tf_op jit(solution)/shard_map/ppermute | solution.py:201
  5.2 2.2 %copy-done = f32[1,1024,1024]{2,1,0:T(8,128)S(1)} copy-done((f32[1,1024,1024]{2,1,0:T(8,128)S(1)}, f32[1,1024,1024]{2,1,0:T(8,128)}, u32[]{:S(2)}) %copy-start) | copy-done | bytes 4194328
  7.4 1.6 %shard_map.50 = (bf16[1024,1024]{1,0:T(8,128)(2,1)S(1)}, bf16[1024,1024]{1,0:T(8,128)(2,1)S(1)}, f32[256,1024]{1,0:T(8,128)S(1)}) custom-call(f32[1024,1024]{1,0:T(8,128)S(1)} %bitcast.8, f32[1024,256]{1,0:T(8,128)S(1)} %bitcast.9), custom_call_target="tpu_custom_call" | custom-call | bytes 10485760 | tf_op jit(solution)/shard_map/pallas_call | solution.py:25
  9.0 5.6 %collective-permute-done.x_ref = f32[64,1024]{1,0:T(8,128)S(1)} collective-permute-done((f32[64,1024]{1,0:T(8,128)S(1)}, f32[64,1024]{1,0:T(8,128)S(1)}, u32[]{:S(2)}, u32[]{:S(2)}) %collective-permute-start) | collective-permute-done | bytes 262176 | tf_op jit(solution)/shard_map/ppermute | solution.py:201
  14.6 0.8 shard_map.51.refs_0_
  15.3 0.7 collective-permute-start.4
  16.0 0.8 shard_map.52.refs_4_
  16.8 9.0 %collective-permute-start.8 = (f32[64,1024]{1,0:T(8,128)S(1)}, f32[64,1024]{1,0:T(8,128)S(1)}, u32[]{:S(2)}, u32[]{:S(2)}) collective-permute-start(f32[64,1024]{1,0:T(8,128)S(1)} %shard_map.52.refs_4_), channel_id=1, source_target_pairs={{8,12},{12,16},{16,20},{20,24},{24,28},{28,8},{0,4},{4,0},{9,13},{... | collective-permute-start | bytes 786440 | tf_op jit(solution)/shard_map/ppermute | solution.py:201
  25.8 4.7 %collective-permute-done.8.x_ref = f32[64,1024]{1,0:T(8,128)S(1)} collective-permute-done((f32[64,1024]{1,0:T(8,128)S(1)}, f32[64,1024]{1,0:T(8,128)S(1)}, u32[]{:S(2)}, u32[]{:S(2)}) %collective-permute-start.8) | collective-permute-done | bytes 262176 | tf_op jit(solution)/shard_map/ppermute | solution.py:201
  30.5 0.8 shard_map.53.refs_8_
  31.3 3.7 %collective-permute-start.12 = (f32[64,1024]{1,0:T(8,128)S(1)}, f32[64,1024]{1,0:T(8,128)S(1)}, u32[]{:S(2)}, u32[]{:S(2)}) collective-permute-start(f32[64,1024]{1,0:T(8,128)S(1)} %shard_map.53.refs_8_), channel_id=1, source_target_pairs={{12,16},{16,20},{20,24},{24,28},{28,12},{0,4},{4,0},{8,8},{13,17},... | collective-permute-start | bytes 786440 | tf_op jit(solution)/shard_map/ppermute | solution.py:201
  34.9 4.7 %collective-permute-done.12.x_ref = f32[64,1024]{1,0:T(8,128)S(1)} collective-permute-done((f32[64,1024]{1,0:T(8,128)S(1)}, f32[64,1024]{1,0:T(8,128)S(1)}, u32[]{:S(2)}, u32[]{:S(2)}) %collective-permute-start.12) | collective-permute-done | bytes 262176 | tf_op jit(solution)/shard_map/ppermute | solution.py:201
  39.6 0.8 shard_map.54.refs_12_
  40.4 2.1 %collective-permute-start.16 = (f32[64,1024]{1,0:T(8,128)S(1)}, f32[64,1024]{1,0:T(8,128)S(1)}, u32[]{:S(2)}, u32[]{:S(2)}) collective-permute-start(f32[64,1024]{1,0:T(8,128)S(1)} %shard_map.54.refs_12_), channel_id=1, source_target_pairs={{16,20},{20,24},{24,28},{28,16},{0,4},{4,0},{8,12},{12,8},{17,21},... | collective-permute-start | bytes 786440 | tf_op jit(solution)/shard_map/ppermute | solution.py:201
  42.5 1.5 %collective-permute-start.2 = (f32[64,1024]{1,0:T(8,128)S(1)}, f32[64,1024]{1,0:T(8,128)S(1)}, u32[]{:S(2)}, u32[]{:S(2)}) collective-permute-start(f32[64,1024]{1,0:T(8,128)S(1)} %shard_map.51.refs_0_), channel_id=1, source_target_pairs={{0,2},{1,3},{2,0},{3,1},{4,6},{5,7},{6,4},{7,5},{8,10},{9,11},{10,... | collective-permute-start | bytes 786440 | tf_op jit(solution)/shard_map/ppermute | solution.py:181
  44.0 2.8 %collective-permute-done.16.x_ref = f32[64,1024]{1,0:T(8,128)S(1)} collective-permute-done((f32[64,1024]{1,0:T(8,128)S(1)}, f32[64,1024]{1,0:T(8,128)S(1)}, u32[]{:S(2)}, u32[]{:S(2)}) %collective-permute-start.16) | collective-permute-done | bytes 262176 | tf_op jit(solution)/shard_map/ppermute | solution.py:201
  46.9 0.8 shard_map.55.refs_16_.refs_0_
  47.7 3.9 %collective-permute-start.20 = (f32[64,1024]{1,0:T(8,128)S(1)}, f32[64,1024]{1,0:T(8,128)S(1)}, u32[]{:S(2)}, u32[]{:S(2)}) collective-permute-start(f32[64,1024]{1,0:T(8,128)S(1)} %shard_map.55.refs_16_.refs_0_), channel_id=1, source_target_pairs={{20,24},{24,28},{28,20},{0,4},{4,0},{8,12},{12,8},{16,16},{21,25},... | collective-permute-start | bytes 786440 | tf_op jit(solution)/shard_map/ppermute | solution.py:201
  51.7 1.6 %collective-permute-start.6 = (f32[64,1024]{1,0:T(8,128)S(1)}, f32[64,1024]{1,0:T(8,128)S(1)}, u32[]{:S(2)}, u32[]{:S(2)}) collective-permute-start(f32[64,1024]{1,0:T(8,128)S(1)} %shard_map.52.refs_4_), channel_id=1, source_target_pairs={{0,2},{1,3},{2,0},{3,1},{4,6},{5,7},{6,4},{7,5},{8,10},{9,11},{10,... | collective-permute-start | bytes 786440 | tf_op jit(solution)/shard_map/ppermute | solution.py:181
  53.8 2.2 %collective-permute-done.20.x_ref = f32[64,1024]{1,0:T(8,128)S(1)} collective-permute-done((f32[64,1024]{1,0:T(8,128)S(1)}, f32[64,1024]{1,0:T(8,128)S(1)}, u32[]{:S(2)}, u32[]{:S(2)}) %collective-permute-start.20) | collective-permute-done | bytes 262176 | tf_op jit(solution)/shard_map/ppermute | solution.py:201
  56.0 1.5 %collective-permute-start.10 = (f32[64,1024]{1,0:T(8,128)S(1)}, f32[64,1024]{1,0:T(8,128)S(1)}, u32[]{:S(2)}, u32[]{:S(2)}) collective-permute-start(f32[64,1024]{1,0:T(8,128)S(1)} %shard_map.53.refs_8_), channel_id=1, source_target_pairs={{0,2},{1,3},{2,0},{3,1},{4,6},{5,7},{6,4},{7,5},{8,10},{9,11},{10,... | collective-permute-start | bytes 786440 | tf_op jit(solution)/shard_map/ppermute | solution.py:181
  57.5 0.8 shard_map.56.refs_20_.refs_4_
  58.4 2.6 %collective-permute-done.6.refs_6_ = f32[64,1024]{1,0:T(8,128)S(1)} collective-permute-done((f32[64,1024]{1,0:T(8,128)S(1)}, f32[64,1024]{1,0:T(8,128)S(1)}, u32[]{:S(2)}, u32[]{:S(2)}) %collective-permute-start.6) | collective-permute-done | bytes 262176 | tf_op jit(solution)/shard_map/ppermute | solution.py:181
  60.9 1.5 %collective-permute-start.14 = (f32[64,1024]{1,0:T(8,128)S(1)}, f32[64,1024]{1,0:T(8,128)S(1)}, u32[]{:S(2)}, u32[]{:S(2)}) collective-permute-start(f32[64,1024]{1,0:T(8,128)S(1)} %shard_map.54.refs_12_), channel_id=1, source_target_pairs={{0,2},{1,3},{2,0},{3,1},{4,6},{5,7},{6,4},{7,5},{8,10},{9,11},{10,... | collective-permute-start | bytes 786440 | tf_op jit(solution)/shard_map/ppermute | solution.py:181
  62.5 0.5 collective-permute-start.18
  63.0 3.6 %collective-permute-done.10.refs_10_ = f32[64,1024]{1,0:T(8,128)S(1)} collective-permute-done((f32[64,1024]{1,0:T(8,128)S(1)}, f32[64,1024]{1,0:T(8,128)S(1)}, u32[]{:S(2)}, u32[]{:S(2)}) %collective-permute-start.10) | collective-permute-done | bytes 262176 | tf_op jit(solution)/shard_map/ppermute | solution.py:181
  66.6 0.6 collective-permute-start.24
  67.7 4.5 %collective-permute-done.14.refs_14_ = f32[64,1024]{1,0:T(8,128)S(1)} collective-permute-done((f32[64,1024]{1,0:T(8,128)S(1)}, f32[64,1024]{1,0:T(8,128)S(1)}, u32[]{:S(2)}, u32[]{:S(2)}) %collective-permute-start.14) | collective-permute-done | bytes 262176 | tf_op jit(solution)/shard_map/ppermute | solution.py:181
  72.2 5.1 %collective-permute-done.18.refs_18_.refs_2_ = f32[64,1024]{1,0:T(8,128)S(1)} collective-permute-done((f32[64,1024]{1,0:T(8,128)S(1)}, f32[64,1024]{1,0:T(8,128)S(1)}, u32[]{:S(2)}, u32[]{:S(2)}) %collective-permute-start.18) | collective-permute-done | bytes 262176 | tf_op jit(solution)/shard_map/ppermute | solution.py:181
  77.8 0.8 shard_map.57.refs_24_.refs_8_
  78.6 1.6 %collective-permute-start.22 = (f32[64,1024]{1,0:T(8,128)S(1)}, f32[64,1024]{1,0:T(8,128)S(1)}, u32[]{:S(2)}, u32[]{:S(2)}) collective-permute-start(f32[64,1024]{1,0:T(8,128)S(1)} %shard_map.56.refs_20_.refs_4_), channel_id=1, source_target_pairs={{0,2},{1,3},{2,0},{3,1},{4,6},{5,7},{6,4},{7,5},{8,10},{9,11},{10,... | collective-permute-start | bytes 786440 | tf_op jit(solution)/shard_map/ppermute | solution.py:181
  80.1 0.5 collective-permute-start.26
  80.7 1.8 %shard_map.59 = (f32[64,512]{1,0:T(8,128)S(1)}, f32[64,512]{1,0:T(8,128)S(1)}, f32[64,512]{1,0:T(8,128)S(1)}, f32[64,512]{1,0:T(8,128)S(1)}, f32[64,512]{1,0:T(8...) custom-call(f32[1,1024]{1,0:T(1,128)S(1)} %copy-done.2, ...), custom_call_target="tpu_custom_call" | custom-call | flops 1610612736 | bytes 7344128 | tf_op jit(solution)/shard_map/pallas_call | solution.py:25
  82.5 1.1 collective-permute-start.32
  83.6 4.2 %collective-permute-done.22.refs_22_.refs_6_ = f32[64,1024]{1,0:T(8,128)S(1)} collective-permute-done((f32[64,1024]{1,0:T(8,128)S(1)}, f32[64,1024]{1,0:T(8,128)S(1)}, u32[]{:S(2)}, u32[]{:S(2)}) %collective-permute-start.22) | collective-permute-done | bytes 262176 | tf_op jit(solution)/shard_map/ppermute | solution.py:181
  88.3 4.1 %collective-permute-done.26.refs_26_.refs_10_ = f32[64,1024]{1,0:T(8,128)S(1)} collective-permute-done((f32[64,1024]{1,0:T(8,128)S(1)}, f32[64,1024]{1,0:T(8,128)S(1)}, u32[]{:S(2)}, u32[]{:S(2)}) %collective-permute-start.26) | collective-permute-done | bytes 262176 | tf_op jit(solution)/shard_map/ppermute | solution.py:181
  93.0 6.3 %collective-permute-done.33.refs_3_ = f32[64,512]{1,0:T(8,128)S(1)} collective-permute-done((f32[64,512]{1,0:T(8,128)S(1)}, f32[64,512]{1,0:T(8,128)S(1)}, u32[]{:S(2)}, u32[]{:S(2)}) %collective-permute-start.33) | collective-permute-done | bytes 131104 | tf_op jit(solution)/shard_map/ppermute | solution.py:181
  99.4 1.1 collective-permute-start.29
  100.4 2.4 %collective-permute-start.30 = (f32[64,512]{1,0:T(8,128)S(1)}, f32[64,512]{1,0:T(8,128)S(1)}, u32[]{:S(2)}, u32[]{:S(2)}) collective-permute-start(f32[64,512]{1,0:T(8,128)S(1)} %get-tuple-element.21), channel_id=1, source_target_pairs={{0,12},{4,8},{8,4},{12,0},{16,28},{20,24},{24,20},{28,16},{1,13},{... | collective-permute-start | bytes 393224 | tf_op jit(solution)/shard_map/ppermute | solution.py:181
  102.9 4.3 %collective-permute-start.34 = (f32[64,512]{1,0:T(8,128)S(1)}, f32[64,512]{1,0:T(8,128)S(1)}, u32[]{:S(2)}, u32[]{:S(2)}) collective-permute-start(f32[64,512]{1,0:T(8,128)S(1)} %shard_map.60), channel_id=1, source_target_pairs={{0,16},{4,20},{8,24},{12,28},{16,0},{20,4},{24,8},{28,12},{1,17},{... | collective-permute-start | bytes 393224 | tf_op jit(solution)/shard_map/ppermute | solution.py:181
  107.2 1.0 shard_map.61
  108.3 1.3 %collective-permute-start.35 = (f32[64,512]{1,0:T(8,128)S(1)}, f32[64,512]{1,0:T(8,128)S(1)}, u32[]{:S(2)}, u32[]{:S(2)}) collective-permute-start(f32[64,512]{1,0:T(8,128)S(1)} %get-tuple-element.26), channel_id=1, source_target_pairs={{28,0},{24,16},{29,4},{25,20},{30,8},{26,24},{31,12},{27,28}} | collective-permute-start | bytes 393224 | tf_op jit(solution)/shard_map/ppermute | solution.py:261
  109.6 1.3 %collective-permute-start.36 = (f32[64,512]{1,0:T(8,128)S(1)}, f32[64,512]{1,0:T(8,128)S(1)}, u32[]{:S(2)}, u32[]{:S(2)}) collective-permute-start(f32[64,512]{1,0:T(8,128)S(1)} %get-tuple-element.27), channel_id=1, source_target_pairs={{28,16},{24,0},{29,20},{25,4},{30,24},{26,8},{31,28},{27,12}} | collective-permute-start | bytes 393224 | tf_op jit(solution)/shard_map/ppermute | solution.py:261
  110.9 2.2 %shard_map.58 = f32[1024,512]{1,0:T(8,128)} custom-call(f32[256,1024]{1,0:T(8,128)S(1)} %get-tuple-element.15.start_ref, f32[64,1024]{1,0:T(8,128)S(1)} %shard_map.51.refs_0_, f32[64,1024]{1,0:T(8,128)S(1)} %collective-permute-done.1.refs_1_, f32[64,1024]{1,0:T(8,128)S(1)} %collective-permute-done.2.refs_2_, f32[64,1024]{1,0:T(8,128)S(1)} %collective-permute-done.3.refs_3_, ...), custom_call_target="tpu_custom_call" | custom-call | bytes 10485760 | tf_op jit(solution)/shard_map/pallas_call | solution.py:25
  113.1 6.1 %collective-permute-done.35 = f32[64,512]{1,0:T(8,128)S(1)} collective-permute-done((f32[64,512]{1,0:T(8,128)S(1)}, f32[64,512]{1,0:T(8,128)S(1)}, u32[]{:S(2)}, u32[]{:S(2)}) %collective-permute-start.35) | collective-permute-done | bytes 131104 | tf_op jit(solution)/shard_map/ppermute | solution.py:261
  119.2 2.0 %collective-permute-done.36 = f32[64,512]{1,0:T(8,128)S(1)} collective-permute-done((f32[64,512]{1,0:T(8,128)S(1)}, f32[64,512]{1,0:T(8,128)S(1)}, u32[]{:S(2)}, u32[]{:S(2)}) %collective-permute-start.36) | collective-permute-done | bytes 131104 | tf_op jit(solution)/shard_map/ppermute | solution.py:261
  121.2 0.7 add_bitcast_fusion
  (47 shorter events, 3.1 us)
Async XLA Ops:
  0.6 4.6 %copy-start.1 = (f32[1,1024,256]{2,1,0:T(8,128)S(1)}, f32[1,1024,256]{2,1,0:T(8,128)}, u32[]{:S(2)}) copy-start(f32[1,1024,256]{2,1,0:T(8,128)} %param.4) | copy-start | bytes 3145732
  2.2 12.4 %collective-permute-start = (f32[64,1024]{1,0:T(8,128)S(1)}, f32[64,1024]{1,0:T(8,128)S(1)}, u32[]{:S(2)}, u32[]{:S(2)}) collective-permute-start(f32[64,1024]{1,0:T(8,128)S(1)} %bitcast.11), channel_id=1, source_target_pairs={{0,4},{4,8},{8,12},{12,16},{16,20},{20,24},{24,28},{28,0},{1,5},{5... | collective-permute-start | bytes 786440 | tf_op jit(solution)/shard_map/ppermute | solution.py:201
  5.2 2.2 %copy-start = (f32[1,1024,1024]{2,1,0:T(8,128)S(1)}, f32[1,1024,1024]{2,1,0:T(8,128)}, u32[]{:S(2)}) copy-start(f32[1,1024,1024]{2,1,0:T(8,128)} %param.3) | copy-start | bytes 12582916
  15.3 0.7 collective-permute-start.4
  16.8 13.7 %collective-permute-start.8 = (f32[64,1024]{1,0:T(8,128)S(1)}, f32[64,1024]{1,0:T(8,128)S(1)}, u32[]{:S(2)}, u32[]{:S(2)}) collective-permute-start(f32[64,1024]{1,0:T(8,128)S(1)} %shard_map.52.refs_4_), channel_id=1, source_target_pairs={{8,12},{12,16},{16,20},{20,24},{24,28},{28,8},{0,4},{4,0},{9,13},{... | collective-permute-start | bytes 786440 | tf_op jit(solution)/shard_map/ppermute | solution.py:201
  31.3 8.4 %collective-permute-start.12 = (f32[64,1024]{1,0:T(8,128)S(1)}, f32[64,1024]{1,0:T(8,128)S(1)}, u32[]{:S(2)}, u32[]{:S(2)}) collective-permute-start(f32[64,1024]{1,0:T(8,128)S(1)} %shard_map.53.refs_8_), channel_id=1, source_target_pairs={{12,16},{16,20},{20,24},{24,28},{28,12},{0,4},{4,0},{8,8},{13,17},... | collective-permute-start | bytes 786440 | tf_op jit(solution)/shard_map/ppermute | solution.py:201
  40.4 6.4 %collective-permute-start.16 = (f32[64,1024]{1,0:T(8,128)S(1)}, f32[64,1024]{1,0:T(8,128)S(1)}, u32[]{:S(2)}, u32[]{:S(2)}) collective-permute-start(f32[64,1024]{1,0:T(8,128)S(1)} %shard_map.54.refs_12_), channel_id=1, source_target_pairs={{16,20},{20,24},{24,28},{28,16},{0,4},{4,0},{8,12},{12,8},{17,21},... | collective-permute-start | bytes 786440 | tf_op jit(solution)/shard_map/ppermute | solution.py:201
  42.5 10.9 %collective-permute-start.2 = (f32[64,1024]{1,0:T(8,128)S(1)}, f32[64,1024]{1,0:T(8,128)S(1)}, u32[]{:S(2)}, u32[]{:S(2)}) collective-permute-start(f32[64,1024]{1,0:T(8,128)S(1)} %shard_map.51.refs_0_), channel_id=1, source_target_pairs={{0,2},{1,3},{2,0},{3,1},{4,6},{5,7},{6,4},{7,5},{8,10},{9,11},{10,... | collective-permute-start | bytes 786440 | tf_op jit(solution)/shard_map/ppermute | solution.py:181
  47.7 8.3 %collective-permute-start.20 = (f32[64,1024]{1,0:T(8,128)S(1)}, f32[64,1024]{1,0:T(8,128)S(1)}, u32[]{:S(2)}, u32[]{:S(2)}) collective-permute-start(f32[64,1024]{1,0:T(8,128)S(1)} %shard_map.55.refs_16_.refs_0_), channel_id=1, source_target_pairs={{20,24},{24,28},{28,20},{0,4},{4,0},{8,12},{12,8},{16,16},{21,25},... | collective-permute-start | bytes 786440 | tf_op jit(solution)/shard_map/ppermute | solution.py:201
  51.6 6.7 %collective-permute-start.1 = (f32[64,1024]{1,0:T(8,128)S(1)}, f32[64,1024]{1,0:T(8,128)S(1)}, u32[]{:S(2)}, u32[]{:S(2)}) collective-permute-start(f32[64,1024]{1,0:T(8,128)S(1)} %shard_map.51.refs_0_), channel_id=1, source_target_pairs={{0,1},{1,0},{2,3},{3,2},{4,5},{5,4},{6,7},{7,6},{8,9},{9,8},{10,11... | collective-permute-start | bytes 786440 | tf_op jit(solution)/shard_map/ppermute | solution.py:181
  51.7 9.2 %collective-permute-start.6 = (f32[64,1024]{1,0:T(8,128)S(1)}, f32[64,1024]{1,0:T(8,128)S(1)}, u32[]{:S(2)}, u32[]{:S(2)}) collective-permute-start(f32[64,1024]{1,0:T(8,128)S(1)} %shard_map.52.refs_4_), channel_id=1, source_target_pairs={{0,2},{1,3},{2,0},{3,1},{4,6},{5,7},{6,4},{7,5},{8,10},{9,11},{10,... | collective-permute-start | bytes 786440 | tf_op jit(solution)/shard_map/ppermute | solution.py:181
  53.3 7.7 %collective-permute-start.5 = (f32[64,1024]{1,0:T(8,128)S(1)}, f32[64,1024]{1,0:T(8,128)S(1)}, u32[]{:S(2)}, u32[]{:S(2)}) collective-permute-start(f32[64,1024]{1,0:T(8,128)S(1)} %shard_map.52.refs_4_), channel_id=1, source_target_pairs={{0,1},{1,0},{2,3},{3,2},{4,5},{5,4},{6,7},{7,6},{8,9},{9,8},{10,11... | collective-permute-start | bytes 786440 | tf_op jit(solution)/shard_map/ppermute | solution.py:181
  53.4 9.0 %collective-permute-start.3 = (f32[64,1024]{1,0:T(8,128)S(1)}, f32[64,1024]{1,0:T(8,128)S(1)}, u32[]{:S(2)}, u32[]{:S(2)}) collective-permute-start(f32[64,1024]{1,0:T(8,128)S(1)} %collective-permute-done.2.refs_2_), channel_id=1, source_target_pairs={{0,1},{1,0},{2,3},{3,2},{4,5},{5,4},{6,7},{7,6},{8,9},{9,8},{10,11... | collective-permute-start | bytes 786440 | tf_op jit(solution)/shard_map/ppermute | solution.py:181
  56.0 10.6 %collective-permute-start.10 = (f32[64,1024]{1,0:T(8,128)S(1)}, f32[64,1024]{1,0:T(8,128)S(1)}, u32[]{:S(2)}, u32[]{:S(2)}) collective-permute-start(f32[64,1024]{1,0:T(8,128)S(1)} %shard_map.53.refs_8_), channel_id=1, source_target_pairs={{0,2},{1,3},{2,0},{3,1},{4,6},{5,7},{6,4},{7,5},{8,10},{9,11},{10,... | collective-permute-start | bytes 786440 | tf_op jit(solution)/shard_map/ppermute | solution.py:181
  58.3 22.4 %copy-start.2 = (f32[1,1024]{1,0:T(1,128)S(1)}, f32[1,1024]{1,0:T(1,128)}, u32[]{:S(2)}) copy-start(f32[1,1024]{1,0:T(1,128)} %weight_ref.3) | copy-start | bytes 12292
  58.3 8.9 %collective-permute-start.9 = (f32[64,1024]{1,0:T(8,128)S(1)}, f32[64,1024]{1,0:T(8,128)S(1)}, u32[]{:S(2)}, u32[]{:S(2)}) collective-permute-start(f32[64,1024]{1,0:T(8,128)S(1)} %shard_map.53.refs_8_), channel_id=1, source_target_pairs={{0,1},{1,0},{2,3},{3,2},{4,5},{5,4},{6,7},{7,6},{8,9},{9,8},{10,11... | collective-permute-start | bytes 786440 | tf_op jit(solution)/shard_map/ppermute | solution.py:181
  60.9 6.2 %collective-permute-start.7 = (f32[64,1024]{1,0:T(8,128)S(1)}, f32[64,1024]{1,0:T(8,128)S(1)}, u32[]{:S(2)}, u32[]{:S(2)}) collective-permute-start(f32[64,1024]{1,0:T(8,128)S(1)} %collective-permute-done.6.refs_6_), channel_id=1, source_target_pairs={{0,1},{1,0},{2,3},{3,2},{4,5},{5,4},{6,7},{7,6},{8,9},{9,8},{10,11... | collective-permute-start | bytes 786440 | tf_op jit(solution)/shard_map/ppermute | solution.py:181
  60.9 11.2 %collective-permute-start.14 = (f32[64,1024]{1,0:T(8,128)S(1)}, f32[64,1024]{1,0:T(8,128)S(1)}, u32[]{:S(2)}, u32[]{:S(2)}) collective-permute-start(f32[64,1024]{1,0:T(8,128)S(1)} %shard_map.54.refs_12_), channel_id=1, source_target_pairs={{0,2},{1,3},{2,0},{3,1},{4,6},{5,7},{6,4},{7,5},{8,10},{9,11},{10,... | collective-permute-start | bytes 786440 | tf_op jit(solution)/shard_map/ppermute | solution.py:181
  62.5 14.8 %collective-permute-start.18 = (f32[64,1024]{1,0:T(8,128)S(1)}, f32[64,1024]{1,0:T(8,128)S(1)}, u32[]{:S(2)}, u32[]{:S(2)}) collective-permute-start(f32[64,1024]{1,0:T(8,128)S(1)} %shard_map.55.refs_16_.refs_0_), channel_id=1, source_target_pairs={{0,2},{1,3},{2,0},{3,1},{4,6},{5,7},{6,4},{7,5},{8,10},{9,11},{10,... | collective-permute-start | bytes 786440 | tf_op jit(solution)/shard_map/ppermute | solution.py:181
  66.6 10.7 %collective-permute-start.24 = (f32[64,1024]{1,0:T(8,128)S(1)}, f32[64,1024]{1,0:T(8,128)S(1)}, u32[]{:S(2)}, u32[]{:S(2)}) collective-permute-start(f32[64,1024]{1,0:T(8,128)S(1)} %shard_map.56.refs_20_.refs_4_), channel_id=1, source_target_pairs={{24,28},{28,24},{0,4},{4,0},{8,12},{12,8},{16,20},{20,16},{25,29},... | collective-permute-start | bytes 786440 | tf_op jit(solution)/shard_map/ppermute | solution.py:201
  67.2 11.4 %collective-permute-start.13 = (f32[64,1024]{1,0:T(8,128)S(1)}, f32[64,1024]{1,0:T(8,128)S(1)}, u32[]{:S(2)}, u32[]{:S(2)}) collective-permute-start(f32[64,1024]{1,0:T(8,128)S(1)} %shard_map.54.refs_12_), channel_id=1, source_target_pairs={{0,1},{1,0},{2,3},{3,2},{4,5},{5,4},{6,7},{7,6},{8,9},{9,8},{10,11... | collective-permute-start | bytes 786440 | tf_op jit(solution)/shard_map/ppermute | solution.py:181
  67.2 13.0 %collective-permute-start.11 = (f32[64,1024]{1,0:T(8,128)S(1)}, f32[64,1024]{1,0:T(8,128)S(1)}, u32[]{:S(2)}, u32[]{:S(2)}) collective-permute-start(f32[64,1024]{1,0:T(8,128)S(1)} %collective-permute-done.10.refs_10_), channel_id=1, source_target_pairs={{0,1},{1,0},{2,3},{3,2},{4,5},{5,4},{6,7},{7,6},{8,9},{9,8},{10,11... | collective-permute-start | bytes 786440 | tf_op jit(solution)/shard_map/ppermute | solution.py:181
  72.2 8.5 %collective-permute-start.17 = (f32[64,1024]{1,0:T(8,128)S(1)}, f32[64,1024]{1,0:T(8,128)S(1)}, u32[]{:S(2)}, u32[]{:S(2)}) collective-permute-start(f32[64,1024]{1,0:T(8,128)S(1)} %shard_map.55.refs_16_.refs_0_), channel_id=1, source_target_pairs={{0,1},{1,0},{2,3},{3,2},{4,5},{5,4},{6,7},{7,6},{8,9},{9,8},{10,11... | collective-permute-start | bytes 786440 | tf_op jit(solution)/shard_map/ppermute | solution.py:181
  77.3 3.4 %collective-permute-start.15 = (f32[64,1024]{1,0:T(8,128)S(1)}, f32[64,1024]{1,0:T(8,128)S(1)}, u32[]{:S(2)}, u32[]{:S(2)}) collective-permute-start(f32[64,1024]{1,0:T(8,128)S(1)} %collective-permute-done.14.refs_14_), channel_id=1, source_target_pairs={{0,1},{1,0},{2,3},{3,2},{4,5},{5,4},{6,7},{7,6},{8,9},{9,8},{10,11... | collective-permute-start | bytes 786440 | tf_op jit(solution)/shard_map/ppermute | solution.py:181
  77.3 3.4 %collective-permute-start.19 = (f32[64,1024]{1,0:T(8,128)S(1)}, f32[64,1024]{1,0:T(8,128)S(1)}, u32[]{:S(2)}, u32[]{:S(2)}) collective-permute-start(f32[64,1024]{1,0:T(8,128)S(1)} %collective-permute-done.18.refs_18_.refs_2_), channel_id=1, source_target_pairs={{0,1},{1,0},{2,3},{3,2},{4,5},{5,4},{6,7},{7,6},{8,9},{9,8},{10,11... | collective-permute-start | bytes 786440 | tf_op jit(solution)/shard_map/ppermute | solution.py:181
  78.6 9.2 %collective-permute-start.22 = (f32[64,1024]{1,0:T(8,128)S(1)}, f32[64,1024]{1,0:T(8,128)S(1)}, u32[]{:S(2)}, u32[]{:S(2)}) collective-permute-start(f32[64,1024]{1,0:T(8,128)S(1)} %shard_map.56.refs_20_.refs_4_), channel_id=1, source_target_pairs={{0,2},{1,3},{2,0},{3,1},{4,6},{5,7},{6,4},{7,5},{8,10},{9,11},{10,... | collective-permute-start | bytes 786440 | tf_op jit(solution)/shard_map/ppermute | solution.py:181
  80.1 12.3 %collective-permute-start.26 = (f32[64,1024]{1,0:T(8,128)S(1)}, f32[64,1024]{1,0:T(8,128)S(1)}, u32[]{:S(2)}, u32[]{:S(2)}) collective-permute-start(f32[64,1024]{1,0:T(8,128)S(1)} %shard_map.57.refs_24_.refs_8_), channel_id=1, source_target_pairs={{0,2},{1,3},{2,0},{3,1},{4,6},{5,7},{6,4},{7,5},{8,10},{9,11},{10,... | collective-permute-start | bytes 786440 | tf_op jit(solution)/shard_map/ppermute | solution.py:181
  82.5 5.4 %collective-permute-start.31 = (f32[64,512]{1,0:T(8,128)S(1)}, f32[64,512]{1,0:T(8,128)S(1)}, u32[]{:S(2)}, u32[]{:S(2)}) collective-permute-start(f32[64,512]{1,0:T(8,128)S(1)} %get-tuple-element.23), channel_id=1, source_target_pairs={{0,4},{4,0},{8,12},{12,8},{16,20},{20,16},{24,28},{28,24},{1,5},{5... | collective-permute-start | bytes 393224 | tf_op jit(solution)/shard_map/ppermute | solution.py:181
  82.5 9.9 %collective-permute-start.32 = (f32[64,512]{1,0:T(8,128)S(1)}, f32[64,512]{1,0:T(8,128)S(1)}, u32[]{:S(2)}, u32[]{:S(2)}) collective-permute-start(f32[64,512]{1,0:T(8,128)S(1)} %get-tuple-element.24), channel_id=1, source_target_pairs={{0,8},{4,12},{8,0},{12,4},{16,24},{20,28},{24,16},{28,20},{1,9},{5... | collective-permute-start | bytes 393224 | tf_op jit(solution)/shard_map/ppermute | solution.py:181
  83.6 15.7 %collective-permute-start.21 = (f32[64,1024]{1,0:T(8,128)S(1)}, f32[64,1024]{1,0:T(8,128)S(1)}, u32[]{:S(2)}, u32[]{:S(2)}) collective-permute-start(f32[64,1024]{1,0:T(8,128)S(1)} %shard_map.56.refs_20_.refs_4_), channel_id=1, source_target_pairs={{0,1},{1,0},{2,3},{3,2},{4,5},{5,4},{6,7},{7,6},{8,9},{9,8},{10,11... | collective-permute-start | bytes 786440 | tf_op jit(solution)/shard_map/ppermute | solution.py:181
  87.8 12.6 %collective-permute-start.25 = (f32[64,1024]{1,0:T(8,128)S(1)}, f32[64,1024]{1,0:T(8,128)S(1)}, u32[]{:S(2)}, u32[]{:S(2)}) collective-permute-start(f32[64,1024]{1,0:T(8,128)S(1)} %shard_map.57.refs_24_.refs_8_), channel_id=1, source_target_pairs={{0,1},{1,0},{2,3},{3,2},{4,5},{5,4},{6,7},{7,6},{8,9},{9,8},{10,11... | collective-permute-start | bytes 786440 | tf_op jit(solution)/shard_map/ppermute | solution.py:181
  87.8 15.1 %collective-permute-start.23 = (f32[64,1024]{1,0:T(8,128)S(1)}, f32[64,1024]{1,0:T(8,128)S(1)}, u32[]{:S(2)}, u32[]{:S(2)}) collective-permute-start(f32[64,1024]{1,0:T(8,128)S(1)} %collective-permute-done.22.refs_22_.refs_6_), channel_id=1, source_target_pairs={{0,1},{1,0},{2,3},{3,2},{4,5},{5,4},{6,7},{7,6},{8,9},{9,8},{10,11... | collective-permute-start | bytes 786440 | tf_op jit(solution)/shard_map/ppermute | solution.py:181
  92.5 14.8 %collective-permute-start.27 = (f32[64,1024]{1,0:T(8,128)S(1)}, f32[64,1024]{1,0:T(8,128)S(1)}, u32[]{:S(2)}, u32[]{:S(2)}) collective-permute-start(f32[64,1024]{1,0:T(8,128)S(1)} %collective-permute-done.26.refs_26_.refs_10_), channel_id=1, source_target_pairs={{0,1},{1,0},{2,3},{3,2},{4,5},{5,4},{6,7},{7,6},{8,9},{9,8},{10,11... | collective-permute-start | bytes 786440 | tf_op jit(solution)/shard_map/ppermute | solution.py:181
  92.5 6.8 %collective-permute-start.33 = (f32[64,512]{1,0:T(8,128)S(1)}, f32[64,512]{1,0:T(8,128)S(1)}, u32[]{:S(2)}, u32[]{:S(2)}) collective-permute-start(f32[64,512]{1,0:T(8,128)S(1)} %get-tuple-element.25), channel_id=1, source_target_pairs={{0,12},{4,8},{8,4},{12,0},{16,28},{20,24},{24,20},{28,16},{1,13},{... | collective-permute-start | bytes 393224 | tf_op jit(solution)/shard_map/ppermute | solution.py:181
  99.3 10.3 %collective-permute-start.28 = (f32[64,512]{1,0:T(8,128)S(1)}, f32[64,512]{1,0:T(8,128)S(1)}, u32[]{:S(2)}, u32[]{:S(2)}) collective-permute-start(f32[64,512]{1,0:T(8,128)S(1)} %get-tuple-element.19), channel_id=1, source_target_pairs={{0,4},{4,0},{8,12},{12,8},{16,20},{20,16},{24,28},{28,24},{1,5},{5... | collective-permute-start | bytes 393224 | tf_op jit(solution)/shard_map/ppermute | solution.py:181
  99.4 13.7 %collective-permute-start.29 = (f32[64,512]{1,0:T(8,128)S(1)}, f32[64,512]{1,0:T(8,128)S(1)}, u32[]{:S(2)}, u32[]{:S(2)}) collective-permute-start(f32[64,512]{1,0:T(8,128)S(1)} %get-tuple-element.20), channel_id=1, source_target_pairs={{0,8},{4,12},{8,0},{12,4},{16,24},{20,28},{24,16},{28,20},{1,9},{5... | collective-permute-start | bytes 393224 | tf_op jit(solution)/shard_map/ppermute | solution.py:181
  100.4 12.7 %collective-permute-start.30 = (f32[64,512]{1,0:T(8,128)S(1)}, f32[64,512]{1,0:T(8,128)S(1)}, u32[]{:S(2)}, u32[]{:S(2)}) collective-permute-start(f32[64,512]{1,0:T(8,128)S(1)} %get-tuple-element.21), channel_id=1, source_target_pairs={{0,12},{4,8},{8,4},{12,0},{16,28},{20,24},{24,20},{28,16},{1,13},{... | collective-permute-start | bytes 393224 | tf_op jit(solution)/shard_map/ppermute | solution.py:181
  102.9 10.2 %collective-permute-start.34 = (f32[64,512]{1,0:T(8,128)S(1)}, f32[64,512]{1,0:T(8,128)S(1)}, u32[]{:S(2)}, u32[]{:S(2)}) collective-permute-start(f32[64,512]{1,0:T(8,128)S(1)} %shard_map.60), channel_id=1, source_target_pairs={{0,16},{4,20},{8,24},{12,28},{16,0},{20,4},{24,8},{28,12},{1,17},{... | collective-permute-start | bytes 393224 | tf_op jit(solution)/shard_map/ppermute | solution.py:181
  108.3 11.0 %collective-permute-start.35 = (f32[64,512]{1,0:T(8,128)S(1)}, f32[64,512]{1,0:T(8,128)S(1)}, u32[]{:S(2)}, u32[]{:S(2)}) collective-permute-start(f32[64,512]{1,0:T(8,128)S(1)} %get-tuple-element.26), channel_id=1, source_target_pairs={{28,0},{24,16},{29,4},{25,20},{30,8},{26,24},{31,12},{27,28}} | collective-permute-start | bytes 393224 | tf_op jit(solution)/shard_map/ppermute | solution.py:261
  109.6 11.6 %collective-permute-start.36 = (f32[64,512]{1,0:T(8,128)S(1)}, f32[64,512]{1,0:T(8,128)S(1)}, u32[]{:S(2)}, u32[]{:S(2)}) collective-permute-start(f32[64,512]{1,0:T(8,128)S(1)} %get-tuple-element.27), channel_id=1, source_target_pairs={{28,16},{24,0},{29,20},{25,4},{30,24},{26,8},{31,28},{27,12}} | collective-permute-start | bytes 393224 | tf_op jit(solution)/shard_map/ppermute | solution.py:261

commit v2 on v1

--- a/solution.py
+++ b/solution.py
@@ -53,15 +53,17 @@
         low_ref[:, i : i + 128] = low.T
 
 
-def step_kernel(x_ref, high_ref, low_ref, y_ref):
-    rows = x_ref.shape[0]
-    high, low = split(x_ref[...])
-    both = jnp.concatenate([high, low], axis=0)
-    for col in range(0, y_ref.shape[1], 256):
-        at = slice(col, col + 256)
-        first = jnp.dot(both, high_ref[:, at], preferred_element_type=F32)
-        second = jnp.dot(high, low_ref[:, at], preferred_element_type=F32)
-        y_ref[:, at] = first[:rows] + (first[rows:] + second)
+def step_kernel(tick, x_ref, high_ref, low_ref, y_ref):
+    @pl.when(lax.axis_index("seg") >= tick)
+    def _():
+        rows = x_ref.shape[0]
+        high, low = split(x_ref[...])
+        both = jnp.concatenate([high, low], axis=0)
+        for col in range(0, y_ref.shape[1], 256):
+            at = slice(col, col + 256)
+            first = jnp.dot(both, high_ref[:, at], preferred_element_type=F32)
+            second = jnp.dot(high, low_ref[:, at], preferred_element_type=F32)
+            y_ref[:, at] = first[:rows] + (first[rows:] + second)
 
 
 def gram3(left_high, left_low, right_high, right_low):
@@ -139,25 +141,38 @@
     pieces = len(layout.ticks) * layout.nctl
     piece_refs, out_refs = refs[:pieces], refs[pieces:-3]
     sens, high, low = refs[-3:]
-    layout.gather(sens, 0, None, piece_refs, nseg)
-    seg = lax.axis_index("seg")
-    own = pl.multiple_of(lax.axis_index("ctl") * width, width)
-    for i in range(0, sens.shape[0], 128):
-        high[i : i + 128, :], low[i : i + 128, :] = split(sens[i : i + 128, :])
-    both = jnp.concatenate([sens[pl.ds(own, width), :], sens[pl.ds(own + nu, width), :]], axis=0)
-    own_high, own_low = split(both * weight_ref[...])
-    left = gram3(own_high, own_low, high[:nu, :], low[:nu, :])
-    right = gram3(own_high, own_low, high[nu:, :], low[nu:, :])
-    rows = out_refs[0].shape[0]
-    last = seg == nseg - 1
-    second_late = (seg - layout.stride) >= nseg - 2
-    for i in range(layout.stride):
-        at = slice(i * rows, (i + 1) * rows)
-        to = slice(width + i * rows, width + (i + 1) * rows)
-        upper = jnp.concatenate([left[at], right[at]], axis=1)
-        lower = jnp.concatenate([left[to], jnp.where(second_late, right[to], 0.0)], axis=1)
-        out_refs[2 * i][...] = jnp.where(last, upper, lower)
-        out_refs[2 * i + 1][...] = jnp.where(last, lower, upper)
+
+    @pl.when(lax.axis_index("seg") >= nseg - 2)
+    def _():
+        layout.gather(sens, 0, None, piece_refs, nseg)
+        seg = lax.axis_index("seg")
+        own = pl.multiple_of(lax.axis_index("ctl") * width, width)
+        for i in range(0, sens.shape[0], 128):
+            high[i : i + 128, :], low[i : i + 128, :] = split(sens[i : i + 128, :])
+        both = jnp.concatenate([sens[pl.ds(own, width), :], sens[pl.ds(own + nu, width), :]], axis=0)
+        own_high, own_low = split(both * weight_ref[...])
+        left = gram3(own_high, own_low, high[:nu, :], low[:nu, :])
+        right = gram3(own_high, own_low, high[nu:, :], low[nu:, :])
+        rows = out_refs[0].shape[0]
+        last = seg == nseg - 1
+        second_late = (seg - layout.stride) >= nseg - 2
+        for i in range(layout.stride):
+            at = slice(i * rows, (i + 1) * rows)
+            to = slice(width + i * rows, width + (i + 1) * rows)
+            upper = jnp.concatenate([left[at], right[at]], axis=1)
+            lower = jnp.concatenate([left[to], jnp.where(second_late, right[to], 0.0)], axis=1)
+            out_refs[2 * i][...] = jnp.where(last, upper, lower)
+            out_refs[2 * i + 1][...] = jnp.where(last, lower, upper)
+
+
+def finish_kernel(early_terms, *refs):
+    *term_refs, sum_ref = refs
+    total = sum(ref[...] for ref in term_refs[:early_terms])
+    sum_ref[...] = total
+
+    @pl.when(lax.axis_index("ctl") == 0)
+    def _():
+        sum_ref[...] = total + sum(ref[...] for ref in term_refs[early_terms:])
 
 
 def place_kernel(layout, start_ref, *refs):
@@ -169,10 +184,12 @@
             sens_ref[k : k + 128, i : i + 128] = sens[i : i + 128, k : k + 128].T
 
 
-def wave_pairs(nseg, tick):
-    pairs = [(i, i + 1) for i in range(tick - 1, nseg - 1)] + [(nseg - 1, tick - 1)]
-    idle = tick - 1
-    pairs += [(i, i ^ 1 if (i ^ 1) < idle else i) for i in range(idle)]
+def wave_pairs(nseg, nctl, tick):
+    pairs = []
+    for c in range(nctl):
+        ring = [(s * nctl + c, (s + 1) * nctl + c) for s in range(tick - 1, nseg - 1)]
+        pairs += ring + [((nseg - 1) * nctl + c, (tick - 1) * nctl + c)]
+        pairs += [(s * nctl + c, s * nctl + (c ^ 1)) for s in range(tick - 1)]
     return pairs
 
 
@@ -198,9 +215,14 @@
     pieces = {}
     early = None
     for tick in range(1, nseg):
-        moved = lax.ppermute(newest, "seg", wave_pairs(nseg, tick))
+        moved = lax.ppermute(newest, ("seg", "ctl"), wave_pairs(nseg, nctl, tick))
         (newest,) = call(
-            step_kernel, [out(newest.shape)], moved, high, low, flops=6 * width * nx * nx
+            functools.partial(step_kernel, tick),
+            [out(newest.shape)],
+            moved,
+            high,
+            low,
+            flops=6 * width * nx * nx,
         )
         group = []
         for r in range(nctl // 2):
@@ -237,8 +259,7 @@
         merge_kernel, [out((rows, 2 * nu))], early[half], *[terms[half + r] for r in range(1, half)]
     )
     far = xor_swap(far, "seg", half)
-    total = early[0]
-    terms = [terms[r] for r in range(1, half)] + [far]
+    terms = [early[0]] + [terms[r] for r in range(1, half)] + [far]
 
     late_ticks = sorted({nseg - 1 - stride, nseg - 2 - stride, nseg - 2, nseg - 1})
     body, given = kernel_of(late_kernel, late_ticks)
@@ -250,20 +271,22 @@
         scratch=[pltpu.VMEM(tall, F32)] + [pltpu.VMEM(tall, BF16)] * 2,
         flops=6 * nx * 2 * width * 2 * nu,
     )
+    last = []
     for i in range(stride):
-        for half in range(2):
+        for part in range(2):
             pairs = []
             for c in range(nctl):
-                near = half * (nseg // 2) + c * stride + i
-                other = (1 - half) * (nseg // 2) + c * stride + i
+                near = part * half + c * stride + i
+                other = (1 - part) * half + c * stride + i
                 pairs.append(((nseg - 1) * nctl + c, near * nctl))
                 pairs.append(((nseg - 2) * nctl + c, other * nctl))
-            terms.append(lax.ppermute(late[2 * i + half], ("seg", "ctl"), pairs))
+            last.append(lax.ppermute(late[2 * i + part], ("seg", "ctl"), pairs))
 
     body, given = kernel_of(place_kernel, list(range(1, nseg)))
     (sens,) = call(body, [out((nx, 2 * nu))], start, *given, scratch=[pltpu.VMEM(tall, F32)])
-    for term in terms:
-        total = total + term
+    (total,) = call(
+        functools.partial(finish_kernel, len(terms)), [out((rows, 2 * nu))], *terms, *last
+    )
     return (sens[None], total[None])
 
 

time: 122 us -> 117 us (0.959)
  starting transfers between devices: 46 us -> 57.3 us
  waiting for transfers between devices: 58.5 us -> 48.5 us
  Pallas kernels: 12.1 us -> 6.28 us
    ppermute x28, starting transfers between devices: 20.4 us -> 51.1 us  [xor_swap(): return lax.ppermute(value, axis, [(i, i ^ by) for i in range(devices)])]
    ppermute x9, starting transfers between devices: 25.6 us -> 6.13 us  [the longest x7 3.56 us: local(): moved = lax.ppermute(newest, ('seg', 'ctl'), wave_pairs(nseg, nctl, tick))]
    ppermute x9, waiting for transfers between devices: 28.1 us -> 19.1 us  [the longest x7 9.93 us: local(): moved = lax.ppermute(newest, ('seg', 'ctl'), wave_pairs(nseg, nctl, tick))]
    pallas_call x12 -> x13, Pallas kernels: 12.1 us -> 6.28 us  [call(): pl.pallas_call(kernel, out_shape=outs, in_specs=[VMEM] * len(args), out_s...]
  transfers between devices with their start and end apart: 37 -> 37, of which waited for: 14 -> 13; matrix products, arithmetic and copies ran while one was open for 0% -> 0% of each run, Pallas kernels for 7% -> 5%
where the time goes in v2:
time: 117 us; the launch traced here: 116 us
  starting transfers between devices  57.3 us (49%)
  waiting for transfers between devices  48.5 us (41%)
  Pallas kernels  6.28 us (5%)
  local copies, waits for them, and re-layouts  3.71 us (3%)
    ppermute x28, starting transfers between devices, xor_swap(): return lax.ppermute(value, axis, [(i, i ^ by) for i in range(devices)])  51.1 us
    ppermute x28, waiting for transfers between devices, xor_swap(): return lax.ppermute(value, axis, [(i, i ^ by) for i in range(devices)])  29.4 us
    ppermute x7, waiting for transfers between devices, local(): moved = lax.ppermute(newest, ('seg', 'ctl'), wave_pairs(nseg, nctl, tick))  9.93 us
    ppermute x2, waiting for transfers between devices, local(): last.append(lax.ppermute(late[2 * i + part], ('seg', 'ctl'), pairs))  9.15 us
    pallas_call x13, Pallas kernels, call(): pl.pallas_call(kernel, out_shape=outs, in_specs=[VMEM] * len(args), out_s...  6.28 us
    ppermute x7, starting transfers between devices, local(): moved = lax.ppermute(newest, ('seg', 'ctl'), wave_pairs(nseg, nctl, tick))  3.56 us
    ppermute x2, starting transfers between devices, local(): last.append(lax.ppermute(late[2 * i + part], ('seg', 'ctl'), pairs))  2.57 us
  transfers between devices with their start and end apart: 37, of which 13 were waited for; matrix products, arithmetic and copies ran while one was open for 0% of the time, Pallas kernels for 5%

profile of v2, /device:TPU:0, one launch (start us, length us, event | category | flops | bytes accessed | tf_op | source)
XLA Modules:
  0.0 116.5 jit_solution(7607952014324861883)
XLA Ops:
  0.6 1.3 %constant_dynamic-slice_fusion = f32[1,1024,64]{2,1,0:T(8,128)S(1)} fusion(f32[1,1024,256]{2,1,0:T(8,128)} %param.4, s32[]{:T(128)S(6)} %select_n.3), kind=kLoop, calls=%fused_computation | loop fusion | bytes 524292 | tf_op jit(solution)/shard_map/dynamic_slice | solution.py:210
  2.0 0.2 copy.5
  2.2 3.0 %collective-permute-start = (f32[64,1024]{1,0:T(8,128)S(1)}, f32[64,1024]{1,0:T(8,128)S(1)}, u32[]{:S(2)}, u32[]{:S(2)}) collective-permute-start(f32[64,1024]{1,0:T(8,128)S(1)} %bitcast.10), channel_id=1, source_target_pairs={{0,4},{4,8},{8,12},{12,16},{16,20},{20,24},{24,28},{28,0},{1,5},{5... | collective-permute-start | bytes 786440 | tf_op jit(solution)/shard_map/ppermute | solution.py:218
  5.2 2.2 %copy-done = f32[1,1024,1024]{2,1,0:T(8,128)S(1)} copy-done((f32[1,1024,1024]{2,1,0:T(8,128)S(1)}, f32[1,1024,1024]{2,1,0:T(8,128)}, u32[]{:S(2)}) %copy-start) | copy-done | bytes 4194328
  7.4 1.6 %shard_map.50 = (bf16[1024,1024]{1,0:T(8,128)(2,1)S(1)}, bf16[1024,1024]{1,0:T(8,128)(2,1)S(1)}, f32[256,1024]{1,0:T(8,128)S(1)}) custom-call(f32[1024,1024]{1,0:T(8,128)S(1)} %bitcast.7, f32[1024,256]{1,0:T(8,128)S(1)} %bitcast.8), custom_call_target="tpu_custom_call" | custom-call | bytes 10485760 | tf_op jit(solution)/shard_map/pallas_call | solution.py:25
  9.0 5.6 %collective-permute-done.x_ref = f32[64,1024]{1,0:T(8,128)S(1)} collective-permute-done((f32[64,1024]{1,0:T(8,128)S(1)}, f32[64,1024]{1,0:T(8,128)S(1)}, u32[]{:S(2)}, u32[]{:S(2)}) %collective-permute-start) | collective-permute-done | bytes 262176 | tf_op jit(solution)/shard_map/ppermute | solution.py:218
  14.6 1.5 %collective-permute-done.4.x_ref = f32[64,1024]{1,0:T(8,128)S(1)} collective-permute-done((f32[64,1024]{1,0:T(8,128)S(1)}, f32[64,1024]{1,0:T(8,128)S(1)}, u32[]{:S(2)}, u32[]{:S(2)}) %collective-permute-start.4) | collective-permute-done | bytes 262176 | tf_op jit(solution)/shard_map/ppermute | solution.py:218
  16.1 0.1 collective-permute-start.8
  16.2 1.4 %collective-permute-done.8.x_ref = f32[64,1024]{1,0:T(8,128)S(1)} collective-permute-done((f32[64,1024]{1,0:T(8,128)S(1)}, f32[64,1024]{1,0:T(8,128)S(1)}, u32[]{:S(2)}, u32[]{:S(2)}) %collective-permute-start.8) | collective-permute-done | bytes 262176 | tf_op jit(solution)/shard_map/ppermute | solution.py:218
  17.6 0.1 collective-permute-start.12
  17.8 1.4 %collective-permute-done.12.x_ref = f32[64,1024]{1,0:T(8,128)S(1)} collective-permute-done((f32[64,1024]{1,0:T(8,128)S(1)}, f32[64,1024]{1,0:T(8,128)S(1)}, u32[]{:S(2)}, u32[]{:S(2)}) %collective-permute-start.12) | collective-permute-done | bytes 262176 | tf_op jit(solution)/shard_map/ppermute | solution.py:218
  19.2 0.1 collective-permute-start.16
  19.3 1.5 %collective-permute-start.2 = (f32[64,1024]{1,0:T(8,128)S(1)}, f32[64,1024]{1,0:T(8,128)S(1)}, u32[]{:S(2)}, u32[]{:S(2)}) collective-permute-start(f32[64,1024]{1,0:T(8,128)S(1)} %shard_map.51.refs_0_), channel_id=1, source_target_pairs={{0,2},{1,3},{2,0},{3,1},{4,6},{5,7},{6,4},{7,5},{8,10},{9,11},{10,... | collective-permute-start | bytes 786440 | tf_op jit(solution)/shard_map/ppermute | solution.py:198
  20.8 0.1 collective-permute-start.20
  20.9 0.4 collective-permute-start.1
  21.3 1.4 %collective-permute-start.6 = (f32[64,1024]{1,0:T(8,128)S(1)}, f32[64,1024]{1,0:T(8,128)S(1)}, u32[]{:S(2)}, u32[]{:S(2)}) collective-permute-start(f32[64,1024]{1,0:T(8,128)S(1)} %shard_map.52.refs_4_), channel_id=1, source_target_pairs={{0,2},{1,3},{2,0},{3,1},{4,6},{5,7},{6,4},{7,5},{8,10},{9,11},{10,... | collective-permute-start | bytes 786440 | tf_op jit(solution)/shard_map/ppermute | solution.py:198
  22.7 5.8 %collective-permute-done.2.refs_2_ = f32[64,1024]{1,0:T(8,128)S(1)} collective-permute-done((f32[64,1024]{1,0:T(8,128)S(1)}, f32[64,1024]{1,0:T(8,128)S(1)}, u32[]{:S(2)}, u32[]{:S(2)}) %collective-permute-start.2) | collective-permute-done | bytes 262176 | tf_op jit(solution)/shard_map/ppermute | solution.py:198
  28.5 1.5 %collective-permute-start.10 = (f32[64,1024]{1,0:T(8,128)S(1)}, f32[64,1024]{1,0:T(8,128)S(1)}, u32[]{:S(2)}, u32[]{:S(2)}) collective-permute-start(f32[64,1024]{1,0:T(8,128)S(1)} %shard_map.53.refs_8_), channel_id=1, source_target_pairs={{0,2},{1,3},{2,0},{3,1},{4,6},{5,7},{6,4},{7,5},{8,10},{9,11},{10,... | collective-permute-start | bytes 786440 | tf_op jit(solution)/shard_map/ppermute | solution.py:198
  30.0 0.2 collective-permute-start.9
  30.2 3.9 %collective-permute-done.6.refs_6_ = f32[64,1024]{1,0:T(8,128)S(1)} collective-permute-done((f32[64,1024]{1,0:T(8,128)S(1)}, f32[64,1024]{1,0:T(8,128)S(1)}, u32[]{:S(2)}, u32[]{:S(2)}) %collective-permute-start.6) | collective-permute-done | bytes 262176 | tf_op jit(solution)/shard_map/ppermute | solution.py:198
  34.1 1.5 %collective-permute-start.14 = (f32[64,1024]{1,0:T(8,128)S(1)}, f32[64,1024]{1,0:T(8,128)S(1)}, u32[]{:S(2)}, u32[]{:S(2)}) collective-permute-start(f32[64,1024]{1,0:T(8,128)S(1)} %shard_map.54.refs_12_), channel_id=1, source_target_pairs={{0,2},{1,3},{2,0},{3,1},{4,6},{5,7},{6,4},{7,5},{8,10},{9,11},{10,... | collective-permute-start | bytes 786440 | tf_op jit(solution)/shard_map/ppermute | solution.py:198
  35.6 0.5 collective-permute-start.18
  36.1 3.6 %collective-permute-done.10.refs_10_ = f32[64,1024]{1,0:T(8,128)S(1)} collective-permute-done((f32[64,1024]{1,0:T(8,128)S(1)}, f32[64,1024]{1,0:T(8,128)S(1)}, u32[]{:S(2)}, u32[]{:S(2)}) %collective-permute-start.10) | collective-permute-done | bytes 262176 | tf_op jit(solution)/shard_map/ppermute | solution.py:198
  39.7 0.5 collective-permute-start.13
  40.2 0.1 collective-permute-start.11
  40.3 5.0 %collective-permute-done.14.refs_14_ = f32[64,1024]{1,0:T(8,128)S(1)} collective-permute-done((f32[64,1024]{1,0:T(8,128)S(1)}, f32[64,1024]{1,0:T(8,128)S(1)}, u32[]{:S(2)}, u32[]{:S(2)}) %collective-permute-start.14) | collective-permute-done | bytes 262176 | tf_op jit(solution)/shard_map/ppermute | solution.py:198
  45.3 5.0 %collective-permute-done.18.refs_18_.refs_2_ = f32[64,1024]{1,0:T(8,128)S(1)} collective-permute-done((f32[64,1024]{1,0:T(8,128)S(1)}, f32[64,1024]{1,0:T(8,128)S(1)}, u32[]{:S(2)}, u32[]{:S(2)}) %collective-permute-start.18) | collective-permute-done | bytes 262176 | tf_op jit(solution)/shard_map/ppermute | solution.py:198
  50.4 0.5 collective-permute-start.19
  50.9 1.5 %collective-permute-start.22 = (f32[64,1024]{1,0:T(8,128)S(1)}, f32[64,1024]{1,0:T(8,128)S(1)}, u32[]{:S(2)}, u32[]{:S(2)}) collective-permute-start(f32[64,1024]{1,0:T(8,128)S(1)} %shard_map.56.refs_20_.refs_4_), channel_id=1, source_target_pairs={{0,2},{1,3},{2,0},{3,1},{4,6},{5,7},{6,4},{7,5},{8,10},{9,11},{10,... | collective-permute-start | bytes 786440 | tf_op jit(solution)/shard_map/ppermute | solution.py:198
  52.4 0.5 collective-permute-start.26
  52.9 1.8 %shard_map.59 = (f32[64,512]{1,0:T(8,128)S(1)}, f32[64,512]{1,0:T(8,128)S(1)}, f32[64,512]{1,0:T(8,128)S(1)}, f32[64,512]{1,0:T(8,128)S(1)}, f32[64,512]{1,0:T(8...) custom-call(f32[1,1024]{1,0:T(1,128)S(1)} %copy-done.2, ...), custom_call_target="tpu_custom_call" | custom-call | flops 1610612736 | bytes 7344128 | tf_op jit(solution)/shard_map/pallas_call | solution.py:25
  54.7 7.1 %collective-permute-start.31 = (f32[64,512]{1,0:T(8,128)S(1)}, f32[64,512]{1,0:T(8,128)S(1)}, u32[]{:S(2)}, u32[]{:S(2)}) collective-permute-start(f32[64,512]{1,0:T(8,128)S(1)} %get-tuple-element.23), channel_id=1, source_target_pairs={{0,4},{4,0},{8,12},{12,8},{16,20},{20,16},{24,28},{28,24},{1,5},{5... | collective-permute-start | bytes 393224 | tf_op jit(solution)/shard_map/ppermute | solution.py:198
  61.8 12.8 %collective-permute-start.32 = (f32[64,512]{1,0:T(8,128)S(1)}, f32[64,512]{1,0:T(8,128)S(1)}, u32[]{:S(2)}, u32[]{:S(2)}) collective-permute-start(f32[64,512]{1,0:T(8,128)S(1)} %get-tuple-element.24), channel_id=1, source_target_pairs={{0,8},{4,12},{8,0},{12,4},{16,24},{20,28},{24,16},{28,20},{1,9},{5... | collective-permute-start | bytes 393224 | tf_op jit(solution)/shard_map/ppermute | solution.py:198
  74.6 0.5 collective-permute-start.25
  75.1 0.1 collective-permute-start.23
  75.2 0.4 collective-permute-start.27
  75.7 1.9 %collective-permute-done.32.refs_2_ = f32[64,512]{1,0:T(8,128)S(1)} collective-permute-done((f32[64,512]{1,0:T(8,128)S(1)}, f32[64,512]{1,0:T(8,128)S(1)}, u32[]{:S(2)}, u32[]{:S(2)}) %collective-permute-start.32) | collective-permute-done | bytes 131104 | tf_op jit(solution)/shard_map/ppermute | solution.py:198
  77.6 6.5 %collective-permute-start.33 = (f32[64,512]{1,0:T(8,128)S(1)}, f32[64,512]{1,0:T(8,128)S(1)}, u32[]{:S(2)}, u32[]{:S(2)}) collective-permute-start(f32[64,512]{1,0:T(8,128)S(1)} %get-tuple-element.25), channel_id=1, source_target_pairs={{0,12},{4,8},{8,4},{12,0},{16,28},{20,24},{24,20},{28,16},{1,13},{... | collective-permute-start | bytes 393224 | tf_op jit(solution)/shard_map/ppermute | solution.py:198
  84.1 4.2 %collective-permute-done.33.refs_3_ = f32[64,512]{1,0:T(8,128)S(1)} collective-permute-done((f32[64,512]{1,0:T(8,128)S(1)}, f32[64,512]{1,0:T(8,128)S(1)}, u32[]{:S(2)}, u32[]{:S(2)}) %collective-permute-start.33) | collective-permute-done | bytes 131104 | tf_op jit(solution)/shard_map/ppermute | solution.py:198
  88.3 3.3 %collective-permute-start.29 = (f32[64,512]{1,0:T(8,128)S(1)}, f32[64,512]{1,0:T(8,128)S(1)}, u32[]{:S(2)}, u32[]{:S(2)}) collective-permute-start(f32[64,512]{1,0:T(8,128)S(1)} %get-tuple-element.20), channel_id=1, source_target_pairs={{0,8},{4,12},{8,0},{12,4},{16,24},{20,28},{24,16},{28,20},{1,9},{5... | collective-permute-start | bytes 393224 | tf_op jit(solution)/shard_map/ppermute | solution.py:198
  91.6 0.3 collective-permute-start.30
  91.9 9.9 %collective-permute-start.34 = (f32[64,512]{1,0:T(8,128)S(1)}, f32[64,512]{1,0:T(8,128)S(1)}, u32[]{:S(2)}, u32[]{:S(2)}) collective-permute-start(f32[64,512]{1,0:T(8,128)S(1)} %shard_map.60), channel_id=1, source_target_pairs={{0,16},{4,20},{8,24},{12,28},{16,0},{20,4},{24,8},{28,12},{1,17},{... | collective-permute-start | bytes 393224 | tf_op jit(solution)/shard_map/ppermute | solution.py:198
  101.8 1.3 %collective-permute-start.35 = (f32[64,512]{1,0:T(8,128)S(1)}, f32[64,512]{1,0:T(8,128)S(1)}, u32[]{:S(2)}, u32[]{:S(2)}) collective-permute-start(f32[64,512]{1,0:T(8,128)S(1)} %get-tuple-element.26), channel_id=1, source_target_pairs={{28,0},{24,16},{29,4},{25,20},{30,8},{26,24},{31,12},{27,28}} | collective-permute-start | bytes 393224 | tf_op jit(solution)/shard_map/ppermute | solution.py:283
  103.1 1.3 %collective-permute-start.36 = (f32[64,512]{1,0:T(8,128)S(1)}, f32[64,512]{1,0:T(8,128)S(1)}, u32[]{:S(2)}, u32[]{:S(2)}) collective-permute-start(f32[64,512]{1,0:T(8,128)S(1)} %get-tuple-element.27), channel_id=1, source_target_pairs={{28,16},{24,0},{29,20},{25,4},{30,24},{26,8},{31,28},{27,12}} | collective-permute-start | bytes 393224 | tf_op jit(solution)/shard_map/ppermute | solution.py:283
  104.4 2.2 %shard_map.58 = f32[1024,512]{1,0:T(8,128)} custom-call(f32[256,1024]{1,0:T(8,128)S(1)} %get-tuple-element.15.start_ref, f32[64,1024]{1,0:T(8,128)S(1)} %shard_map.51.refs_0_, f32[64,1024]{1,0:T(8,128)S(1)} %collective-permute-done.1.refs_1_, f32[64,1024]{1,0:T(8,128)S(1)} %collective-permute-done.2.refs_2_, f32[64,1024]{1,0:T(8,128)S(1)} %collective-permute-done.3.refs_3_, ...), custom_call_target="tpu_custom_call" | custom-call | bytes 10485760 | tf_op jit(solution)/shard_map/pallas_call | solution.py:25
  106.6 6.1 %collective-permute-done.35.refs_5_ = f32[64,512]{1,0:T(8,128)S(1)} collective-permute-done((f32[64,512]{1,0:T(8,128)S(1)}, f32[64,512]{1,0:T(8,128)S(1)}, u32[]{:S(2)}, u32[]{:S(2)}) %collective-permute-start.35) | collective-permute-done | bytes 131104 | tf_op jit(solution)/shard_map/ppermute | solution.py:283
  112.8 3.0 %collective-permute-done.36.refs_6_ = f32[64,512]{1,0:T(8,128)S(1)} collective-permute-done((f32[64,512]{1,0:T(8,128)S(1)}, f32[64,512]{1,0:T(8,128)S(1)}, u32[]{:S(2)}, u32[]{:S(2)}) %collective-permute-start.36) | collective-permute-done | bytes 131104 | tf_op jit(solution)/shard_map/ppermute | solution.py:283
  115.8 0.7 shard_map.62
  (47 shorter events, 0.1 us)
Async XLA Ops:
  0.6 4.6 %copy-start.1 = (f32[1,1024,256]{2,1,0:T(8,128)S(1)}, f32[1,1024,256]{2,1,0:T(8,128)}, u32[]{:S(2)}) copy-start(f32[1,1024,256]{2,1,0:T(8,128)} %param.4) | copy-start | bytes 3145732
  2.2 12.4 %collective-permute-start = (f32[64,1024]{1,0:T(8,128)S(1)}, f32[64,1024]{1,0:T(8,128)S(1)}, u32[]{:S(2)}, u32[]{:S(2)}) collective-permute-start(f32[64,1024]{1,0:T(8,128)S(1)} %bitcast.10), channel_id=1, source_target_pairs={{0,4},{4,8},{8,12},{12,16},{16,20},{20,24},{24,28},{28,0},{1,5},{5... | collective-permute-start | bytes 786440 | tf_op jit(solution)/shard_map/ppermute | solution.py:218
  5.2 2.2 %copy-start = (f32[1,1024,1024]{2,1,0:T(8,128)S(1)}, f32[1,1024,1024]{2,1,0:T(8,128)}, u32[]{:S(2)}) copy-start(f32[1,1024,1024]{2,1,0:T(8,128)} %param.3) | copy-start | bytes 12582916
  14.6 1.5 %collective-permute-start.4 = (f32[64,1024]{1,0:T(8,128)S(1)}, f32[64,1024]{1,0:T(8,128)S(1)}, u32[]{:S(2)}, u32[]{:S(2)}) collective-permute-start(f32[64,1024]{1,0:T(8,128)S(1)} %shard_map.51.refs_0_), channel_id=1, source_target_pairs={{4,8},{8,12},{12,16},{16,20},{20,24},{24,28},{28,4},{0,1},{5,9},{9... | collective-permute-start | bytes 786440 | tf_op jit(solution)/shard_map/ppermute | solution.py:218
  16.1 1.5 %collective-permute-start.8 = (f32[64,1024]{1,0:T(8,128)S(1)}, f32[64,1024]{1,0:T(8,128)S(1)}, u32[]{:S(2)}, u32[]{:S(2)}) collective-permute-start(f32[64,1024]{1,0:T(8,128)S(1)} %shard_map.52.refs_4_), channel_id=1, source_target_pairs={{8,12},{12,16},{16,20},{20,24},{24,28},{28,8},{0,1},{4,5},{9,13},{... | collective-permute-start | bytes 786440 | tf_op jit(solution)/shard_map/ppermute | solution.py:218
  17.6 1.5 %collective-permute-start.12 = (f32[64,1024]{1,0:T(8,128)S(1)}, f32[64,1024]{1,0:T(8,128)S(1)}, u32[]{:S(2)}, u32[]{:S(2)}) collective-permute-start(f32[64,1024]{1,0:T(8,128)S(1)} %shard_map.53.refs_8_), channel_id=1, source_target_pairs={{12,16},{16,20},{20,24},{24,28},{28,12},{0,1},{4,5},{8,9},{13,17},... | collective-permute-start | bytes 786440 | tf_op jit(solution)/shard_map/ppermute | solution.py:218
  19.2 1.6 %collective-permute-start.16 = (f32[64,1024]{1,0:T(8,128)S(1)}, f32[64,1024]{1,0:T(8,128)S(1)}, u32[]{:S(2)}, u32[]{:S(2)}) collective-permute-start(f32[64,1024]{1,0:T(8,128)S(1)} %shard_map.54.refs_12_), channel_id=1, source_target_pairs={{16,20},{20,24},{24,28},{28,16},{0,1},{4,5},{8,9},{12,13},{17,21},... | collective-permute-start | bytes 786440 | tf_op jit(solution)/shard_map/ppermute | solution.py:218
  19.3 9.2 %collective-permute-start.2 = (f32[64,1024]{1,0:T(8,128)S(1)}, f32[64,1024]{1,0:T(8,128)S(1)}, u32[]{:S(2)}, u32[]{:S(2)}) collective-permute-start(f32[64,1024]{1,0:T(8,128)S(1)} %shard_map.51.refs_0_), channel_id=1, source_target_pairs={{0,2},{1,3},{2,0},{3,1},{4,6},{5,7},{6,4},{7,5},{8,10},{9,11},{10,... | collective-permute-start | bytes 786440 | tf_op jit(solution)/shard_map/ppermute | solution.py:198
  20.8 7.7 %collective-permute-start.20 = (f32[64,1024]{1,0:T(8,128)S(1)}, f32[64,1024]{1,0:T(8,128)S(1)}, u32[]{:S(2)}, u32[]{:S(2)}) collective-permute-start(f32[64,1024]{1,0:T(8,128)S(1)} %shard_map.55.refs_16_.refs_0_), channel_id=1, source_target_pairs={{20,24},{24,28},{28,20},{0,1},{4,5},{8,9},{12,13},{16,17},{21,25},... | collective-permute-start | bytes 786440 | tf_op jit(solution)/shard_map/ppermute | solution.py:218
  20.9 9.1 %collective-permute-start.1 = (f32[64,1024]{1,0:T(8,128)S(1)}, f32[64,1024]{1,0:T(8,128)S(1)}, u32[]{:S(2)}, u32[]{:S(2)}) collective-permute-start(f32[64,1024]{1,0:T(8,128)S(1)} %shard_map.51.refs_0_), channel_id=1, source_target_pairs={{0,1},{1,0},{2,3},{3,2},{4,5},{5,4},{6,7},{7,6},{8,9},{9,8},{10,11... | collective-permute-start | bytes 786440 | tf_op jit(solution)/shard_map/ppermute | solution.py:198
  21.3 12.8 %collective-permute-start.6 = (f32[64,1024]{1,0:T(8,128)S(1)}, f32[64,1024]{1,0:T(8,128)S(1)}, u32[]{:S(2)}, u32[]{:S(2)}) collective-permute-start(f32[64,1024]{1,0:T(8,128)S(1)} %shard_map.52.refs_4_), channel_id=1, source_target_pairs={{0,2},{1,3},{2,0},{3,1},{4,6},{5,7},{6,4},{7,5},{8,10},{9,11},{10,... | collective-permute-start | bytes 786440 | tf_op jit(solution)/shard_map/ppermute | solution.py:198
  22.7 11.4 %collective-permute-start.5 = (f32[64,1024]{1,0:T(8,128)S(1)}, f32[64,1024]{1,0:T(8,128)S(1)}, u32[]{:S(2)}, u32[]{:S(2)}) collective-permute-start(f32[64,1024]{1,0:T(8,128)S(1)} %shard_map.52.refs_4_), channel_id=1, source_target_pairs={{0,1},{1,0},{2,3},{3,2},{4,5},{5,4},{6,7},{7,6},{8,9},{9,8},{10,11... | collective-permute-start | bytes 786440 | tf_op jit(solution)/shard_map/ppermute | solution.py:198
  28.5 7.1 %collective-permute-start.3 = (f32[64,1024]{1,0:T(8,128)S(1)}, f32[64,1024]{1,0:T(8,128)S(1)}, u32[]{:S(2)}, u32[]{:S(2)}) collective-permute-start(f32[64,1024]{1,0:T(8,128)S(1)} %collective-permute-done.2.refs_2_), channel_id=1, source_target_pairs={{0,1},{1,0},{2,3},{3,2},{4,5},{5,4},{6,7},{7,6},{8,9},{9,8},{10,11... | collective-permute-start | bytes 786440 | tf_op jit(solution)/shard_map/ppermute | solution.py:198
  28.5 11.2 %collective-permute-start.10 = (f32[64,1024]{1,0:T(8,128)S(1)}, f32[64,1024]{1,0:T(8,128)S(1)}, u32[]{:S(2)}, u32[]{:S(2)}) collective-permute-start(f32[64,1024]{1,0:T(8,128)S(1)} %shard_map.53.refs_8_), channel_id=1, source_target_pairs={{0,2},{1,3},{2,0},{3,1},{4,6},{5,7},{6,4},{7,5},{8,10},{9,11},{10,... | collective-permute-start | bytes 786440 | tf_op jit(solution)/shard_map/ppermute | solution.py:198
  30.0 22.9 %copy-start.2 = (f32[1,1024]{1,0:T(1,128)S(1)}, f32[1,1024]{1,0:T(1,128)}, u32[]{:S(2)}) copy-start(f32[1,1024]{1,0:T(1,128)} %weight_ref.3) | copy-start | bytes 12292
  30.0 9.7 %collective-permute-start.9 = (f32[64,1024]{1,0:T(8,128)S(1)}, f32[64,1024]{1,0:T(8,128)S(1)}, u32[]{:S(2)}, u32[]{:S(2)}) collective-permute-start(f32[64,1024]{1,0:T(8,128)S(1)} %shard_map.53.refs_8_), channel_id=1, source_target_pairs={{0,1},{1,0},{2,3},{3,2},{4,5},{5,4},{6,7},{7,6},{8,9},{9,8},{10,11... | collective-permute-start | bytes 786440 | tf_op jit(solution)/shard_map/ppermute | solution.py:198
  34.1 6.1 %collective-permute-start.7 = (f32[64,1024]{1,0:T(8,128)S(1)}, f32[64,1024]{1,0:T(8,128)S(1)}, u32[]{:S(2)}, u32[]{:S(2)}) collective-permute-start(f32[64,1024]{1,0:T(8,128)S(1)} %collective-permute-done.6.refs_6_), channel_id=1, source_target_pairs={{0,1},{1,0},{2,3},{3,2},{4,5},{5,4},{6,7},{7,6},{8,9},{9,8},{10,11... | collective-permute-start | bytes 786440 | tf_op jit(solution)/shard_map/ppermute | solution.py:198
  34.1 11.2 %collective-permute-start.14 = (f32[64,1024]{1,0:T(8,128)S(1)}, f32[64,1024]{1,0:T(8,128)S(1)}, u32[]{:S(2)}, u32[]{:S(2)}) collective-permute-start(f32[64,1024]{1,0:T(8,128)S(1)} %shard_map.54.refs_12_), channel_id=1, source_target_pairs={{0,2},{1,3},{2,0},{3,1},{4,6},{5,7},{6,4},{7,5},{8,10},{9,11},{10,... | collective-permute-start | bytes 786440 | tf_op jit(solution)/shard_map/ppermute | solution.py:198
  35.6 14.8 %collective-permute-start.18 = (f32[64,1024]{1,0:T(8,128)S(1)}, f32[64,1024]{1,0:T(8,128)S(1)}, u32[]{:S(2)}, u32[]{:S(2)}) collective-permute-start(f32[64,1024]{1,0:T(8,128)S(1)} %shard_map.55.refs_16_.refs_0_), channel_id=1, source_target_pairs={{0,2},{1,3},{2,0},{3,1},{4,6},{5,7},{6,4},{7,5},{8,10},{9,11},{10,... | collective-permute-start | bytes 786440 | tf_op jit(solution)/shard_map/ppermute | solution.py:198
  39.7 10.6 %collective-permute-start.24 = (f32[64,1024]{1,0:T(8,128)S(1)}, f32[64,1024]{1,0:T(8,128)S(1)}, u32[]{:S(2)}, u32[]{:S(2)}) collective-permute-start(f32[64,1024]{1,0:T(8,128)S(1)} %shard_map.56.refs_20_.refs_4_), channel_id=1, source_target_pairs={{24,28},{28,24},{0,1},{4,5},{8,9},{12,13},{16,17},{20,21},{25,29},... | collective-permute-start | bytes 786440 | tf_op jit(solution)/shard_map/ppermute | solution.py:218
  39.7 11.2 %collective-permute-start.13 = (f32[64,1024]{1,0:T(8,128)S(1)}, f32[64,1024]{1,0:T(8,128)S(1)}, u32[]{:S(2)}, u32[]{:S(2)}) collective-permute-start(f32[64,1024]{1,0:T(8,128)S(1)} %shard_map.54.refs_12_), channel_id=1, source_target_pairs={{0,1},{1,0},{2,3},{3,2},{4,5},{5,4},{6,7},{7,6},{8,9},{9,8},{10,11... | collective-permute-start | bytes 786440 | tf_op jit(solution)/shard_map/ppermute | solution.py:198
  40.2 12.1 %collective-permute-start.11 = (f32[64,1024]{1,0:T(8,128)S(1)}, f32[64,1024]{1,0:T(8,128)S(1)}, u32[]{:S(2)}, u32[]{:S(2)}) collective-permute-start(f32[64,1024]{1,0:T(8,128)S(1)} %collective-permute-done.10.refs_10_), channel_id=1, source_target_pairs={{0,1},{1,0},{2,3},{3,2},{4,5},{5,4},{6,7},{7,6},{8,9},{9,8},{10,11... | collective-permute-start | bytes 786440 | tf_op jit(solution)/shard_map/ppermute | solution.py:198
  45.3 7.6 %collective-permute-start.17 = (f32[64,1024]{1,0:T(8,128)S(1)}, f32[64,1024]{1,0:T(8,128)S(1)}, u32[]{:S(2)}, u32[]{:S(2)}) collective-permute-start(f32[64,1024]{1,0:T(8,128)S(1)} %shard_map.55.refs_16_.refs_0_), channel_id=1, source_target_pairs={{0,1},{1,0},{2,3},{3,2},{4,5},{5,4},{6,7},{7,6},{8,9},{9,8},{10,11... | collective-permute-start | bytes 786440 | tf_op jit(solution)/shard_map/ppermute | solution.py:198
  50.4 2.6 %collective-permute-start.15 = (f32[64,1024]{1,0:T(8,128)S(1)}, f32[64,1024]{1,0:T(8,128)S(1)}, u32[]{:S(2)}, u32[]{:S(2)}) collective-permute-start(f32[64,1024]{1,0:T(8,128)S(1)} %collective-permute-done.14.refs_14_), channel_id=1, source_target_pairs={{0,1},{1,0},{2,3},{3,2},{4,5},{5,4},{6,7},{7,6},{8,9},{9,8},{10,11... | collective-permute-start | bytes 786440 | tf_op jit(solution)/shard_map/ppermute | solution.py:198
  50.4 2.6 %collective-permute-start.19 = (f32[64,1024]{1,0:T(8,128)S(1)}, f32[64,1024]{1,0:T(8,128)S(1)}, u32[]{:S(2)}, u32[]{:S(2)}) collective-permute-start(f32[64,1024]{1,0:T(8,128)S(1)} %collective-permute-done.18.refs_18_.refs_2_), channel_id=1, source_target_pairs={{0,1},{1,0},{2,3},{3,2},{4,5},{5,4},{6,7},{7,6},{8,9},{9,8},{10,11... | collective-permute-start | bytes 786440 | tf_op jit(solution)/shard_map/ppermute | solution.py:198
  50.9 23.8 %collective-permute-start.22 = (f32[64,1024]{1,0:T(8,128)S(1)}, f32[64,1024]{1,0:T(8,128)S(1)}, u32[]{:S(2)}, u32[]{:S(2)}) collective-permute-start(f32[64,1024]{1,0:T(8,128)S(1)} %shard_map.56.refs_20_.refs_4_), channel_id=1, source_target_pairs={{0,2},{1,3},{2,0},{3,1},{4,6},{5,7},{6,4},{7,5},{8,10},{9,11},{10,... | collective-permute-start | bytes 786440 | tf_op jit(solution)/shard_map/ppermute | solution.py:198
  52.4 22.8 %collective-permute-start.26 = (f32[64,1024]{1,0:T(8,128)S(1)}, f32[64,1024]{1,0:T(8,128)S(1)}, u32[]{:S(2)}, u32[]{:S(2)}) collective-permute-start(f32[64,1024]{1,0:T(8,128)S(1)} %shard_map.57.refs_24_.refs_8_), channel_id=1, source_target_pairs={{0,2},{1,3},{2,0},{3,1},{4,6},{5,7},{6,4},{7,5},{8,10},{9,11},{10,... | collective-permute-start | bytes 786440 | tf_op jit(solution)/shard_map/ppermute | solution.py:198
  54.7 20.4 %collective-permute-start.31 = (f32[64,512]{1,0:T(8,128)S(1)}, f32[64,512]{1,0:T(8,128)S(1)}, u32[]{:S(2)}, u32[]{:S(2)}) collective-permute-start(f32[64,512]{1,0:T(8,128)S(1)} %get-tuple-element.23), channel_id=1, source_target_pairs={{0,4},{4,0},{8,12},{12,8},{16,20},{20,16},{24,28},{28,24},{1,5},{5... | collective-permute-start | bytes 393224 | tf_op jit(solution)/shard_map/ppermute | solution.py:198
  61.8 15.7 %collective-permute-start.32 = (f32[64,512]{1,0:T(8,128)S(1)}, f32[64,512]{1,0:T(8,128)S(1)}, u32[]{:S(2)}, u32[]{:S(2)}) collective-permute-start(f32[64,512]{1,0:T(8,128)S(1)} %get-tuple-element.24), channel_id=1, source_target_pairs={{0,8},{4,12},{8,0},{12,4},{16,24},{20,28},{24,16},{28,20},{1,9},{5... | collective-permute-start | bytes 393224 | tf_op jit(solution)/shard_map/ppermute | solution.py:198
  74.6 13.7 %collective-permute-start.21 = (f32[64,1024]{1,0:T(8,128)S(1)}, f32[64,1024]{1,0:T(8,128)S(1)}, u32[]{:S(2)}, u32[]{:S(2)}) collective-permute-start(f32[64,1024]{1,0:T(8,128)S(1)} %shard_map.56.refs_20_.refs_4_), channel_id=1, source_target_pairs={{0,1},{1,0},{2,3},{3,2},{4,5},{5,4},{6,7},{7,6},{8,9},{9,8},{10,11... | collective-permute-start | bytes 786440 | tf_op jit(solution)/shard_map/ppermute | solution.py:198
  74.6 16.9 %collective-permute-start.25 = (f32[64,1024]{1,0:T(8,128)S(1)}, f32[64,1024]{1,0:T(8,128)S(1)}, u32[]{:S(2)}, u32[]{:S(2)}) collective-permute-start(f32[64,1024]{1,0:T(8,128)S(1)} %shard_map.57.refs_24_.refs_8_), channel_id=1, source_target_pairs={{0,1},{1,0},{2,3},{3,2},{4,5},{5,4},{6,7},{7,6},{8,9},{9,8},{10,11... | collective-permute-start | bytes 786440 | tf_op jit(solution)/shard_map/ppermute | solution.py:198
  75.1 16.7 %collective-permute-start.23 = (f32[64,1024]{1,0:T(8,128)S(1)}, f32[64,1024]{1,0:T(8,128)S(1)}, u32[]{:S(2)}, u32[]{:S(2)}) collective-permute-start(f32[64,1024]{1,0:T(8,128)S(1)} %collective-permute-done.22.refs_22_.refs_6_), channel_id=1, source_target_pairs={{0,1},{1,0},{2,3},{3,2},{4,5},{5,4},{6,7},{7,6},{8,9},{9,8},{10,11... | collective-permute-start | bytes 786440 | tf_op jit(solution)/shard_map/ppermute | solution.py:198
  75.2 26.6 %collective-permute-start.27 = (f32[64,1024]{1,0:T(8,128)S(1)}, f32[64,1024]{1,0:T(8,128)S(1)}, u32[]{:S(2)}, u32[]{:S(2)}) collective-permute-start(f32[64,1024]{1,0:T(8,128)S(1)} %collective-permute-done.26.refs_26_.refs_10_), channel_id=1, source_target_pairs={{0,1},{1,0},{2,3},{3,2},{4,5},{5,4},{6,7},{7,6},{8,9},{9,8},{10,11... | collective-permute-start | bytes 786440 | tf_op jit(solution)/shard_map/ppermute | solution.py:198
  77.6 10.7 %collective-permute-start.33 = (f32[64,512]{1,0:T(8,128)S(1)}, f32[64,512]{1,0:T(8,128)S(1)}, u32[]{:S(2)}, u32[]{:S(2)}) collective-permute-start(f32[64,512]{1,0:T(8,128)S(1)} %get-tuple-element.25), channel_id=1, source_target_pairs={{0,12},{4,8},{8,4},{12,0},{16,28},{20,24},{24,20},{28,16},{1,13},{... | collective-permute-start | bytes 393224 | tf_op jit(solution)/shard_map/ppermute | solution.py:198
  88.2 14.9 %collective-permute-start.28 = (f32[64,512]{1,0:T(8,128)S(1)}, f32[64,512]{1,0:T(8,128)S(1)}, u32[]{:S(2)}, u32[]{:S(2)}) collective-permute-start(f32[64,512]{1,0:T(8,128)S(1)} %get-tuple-element.19), channel_id=1, source_target_pairs={{0,4},{4,0},{8,12},{12,8},{16,20},{20,16},{24,28},{28,24},{1,5},{5... | collective-permute-start | bytes 393224 | tf_op jit(solution)/shard_map/ppermute | solution.py:198
  88.3 18.3 %collective-permute-start.29 = (f32[64,512]{1,0:T(8,128)S(1)}, f32[64,512]{1,0:T(8,128)S(1)}, u32[]{:S(2)}, u32[]{:S(2)}) collective-permute-start(f32[64,512]{1,0:T(8,128)S(1)} %get-tuple-element.20), channel_id=1, source_target_pairs={{0,8},{4,12},{8,0},{12,4},{16,24},{20,28},{24,16},{28,20},{1,9},{5... | collective-permute-start | bytes 393224 | tf_op jit(solution)/shard_map/ppermute | solution.py:198
  91.6 15.1 %collective-permute-start.30 = (f32[64,512]{1,0:T(8,128)S(1)}, f32[64,512]{1,0:T(8,128)S(1)}, u32[]{:S(2)}, u32[]{:S(2)}) collective-permute-start(f32[64,512]{1,0:T(8,128)S(1)} %get-tuple-element.21), channel_id=1, source_target_pairs={{0,12},{4,8},{8,4},{12,0},{16,28},{20,24},{24,20},{28,16},{1,13},{... | collective-permute-start | bytes 393224 | tf_op jit(solution)/shard_map/ppermute | solution.py:198
  91.9 14.8 %collective-permute-start.34 = (f32[64,512]{1,0:T(8,128)S(1)}, f32[64,512]{1,0:T(8,128)S(1)}, u32[]{:S(2)}, u32[]{:S(2)}) collective-permute-start(f32[64,512]{1,0:T(8,128)S(1)} %shard_map.60), channel_id=1, source_target_pairs={{0,16},{4,20},{8,24},{12,28},{16,0},{20,4},{24,8},{28,12},{1,17},{... | collective-permute-start | bytes 393224 | tf_op jit(solution)/shard_map/ppermute | solution.py:198
  101.8 10.9 %collective-permute-start.35 = (f32[64,512]{1,0:T(8,128)S(1)}, f32[64,512]{1,0:T(8,128)S(1)}, u32[]{:S(2)}, u32[]{:S(2)}) collective-permute-start(f32[64,512]{1,0:T(8,128)S(1)} %get-tuple-element.26), channel_id=1, source_target_pairs={{28,0},{24,16},{29,4},{25,20},{30,8},{26,24},{31,12},{27,28}} | collective-permute-start | bytes 393224 | tf_op jit(solution)/shard_map/ppermute | solution.py:283
  103.1 12.7 %collective-permute-start.36 = (f32[64,512]{1,0:T(8,128)S(1)}, f32[64,512]{1,0:T(8,128)S(1)}, u32[]{:S(2)}, u32[]{:S(2)}) collective-permute-start(f32[64,512]{1,0:T(8,128)S(1)} %get-tuple-element.27), channel_id=1, source_target_pairs={{28,16},{24,0},{29,20},{25,4},{30,24},{26,8},{31,28},{27,12}} | collective-permute-start | bytes 393224 | tf_op jit(solution)/shard_map/ppermute | solution.py:283

commit v3 on v2

--- a/solution.py
+++ b/solution.py
@@ -53,17 +53,37 @@
         low_ref[:, i : i + 128] = low.T
 
 
-def step_kernel(tick, x_ref, high_ref, low_ref, y_ref):
+def product(x, high_ref, low_ref, store):
+    rows = x.shape[0]
+    high, low = split(x)
+    both = jnp.concatenate([high, low], axis=0)
+    for col in range(0, high_ref.shape[1], 256):
+        at = slice(col, col + 256)
+        first = jnp.dot(both, high_ref[:, at], preferred_element_type=F32)
+        second = jnp.dot(high, low_ref[:, at], preferred_element_type=F32)
+        store(at, first[:rows] + (first[rows:] + second))
+
+
+def step_kernel(tick, part, x_ref, high_ref, low_ref, *refs):
     @pl.when(lax.axis_index("seg") >= tick)
     def _():
         rows = x_ref.shape[0]
-        high, low = split(x_ref[...])
-        both = jnp.concatenate([high, low], axis=0)
-        for col in range(0, y_ref.shape[1], 256):
-            at = slice(col, col + 256)
-            first = jnp.dot(both, high_ref[:, at], preferred_element_type=F32)
-            second = jnp.dot(high, low_ref[:, at], preferred_element_type=F32)
-            y_ref[:, at] = first[:rows] + (first[rows:] + second)
+
+        def store(at, y):
+            if part == "whole":
+                whole_ref, first_ref, second_ref = refs
+                whole_ref[:, at] = y
+                first_ref[:, at] = y[: rows // 2]
+                second_ref[:, at] = y[rows // 2 :]
+            elif part == "first":
+                refs[0][:, at] = y
+            else:
+                first_ref, whole_ref, second_ref = refs
+                whole_ref[:rows, at] = first_ref[:, at]
+                whole_ref[rows:, at] = y
+                second_ref[:, at] = y
+
+        product(x_ref[...], high_ref, low_ref, store)
 
 
 def gram3(left_high, left_low, right_high, right_low):
@@ -215,15 +235,24 @@
     pieces = {}
     early = None
     for tick in range(1, nseg):
-        moved = lax.ppermute(newest, ("seg", "ctl"), wave_pairs(nseg, nctl, tick))
-        (newest,) = call(
-            functools.partial(step_kernel, tick),
-            [out(newest.shape)],
-            moved,
-            high,
-            low,
-            flops=6 * width * nx * nx,
-        )
+        def wave(value):
+            return lax.ppermute(value, ("seg", "ctl"), wave_pairs(nseg, nctl, tick))
+
+        def step(part, outs, *args):
+            body = functools.partial(step_kernel, tick, part)
+            flops = 6 * args[0].shape[0] * nx * nx
+            return call(body, [out(shape) for shape in outs], *args, flops=flops)
+
+        part_shape = (width // 2, nx)
+        if tick == 1:
+            moved = wave(newest)
+            newest, upper, lower = step(
+                "whole", [newest.shape, part_shape, part_shape], moved, high, low
+            )
+        else:
+            moved = [wave(upper), wave(lower)]
+            (upper,) = step("first", [part_shape], moved[0], high, low)
+            newest, lower = step("second", [newest.shape, part_shape], moved[1], high, low, upper)
         group = []
         for r in range(nctl // 2):
             here = newest

time: 117 us -> 114 us (0.974)
  starting transfers between devices: 57.3 us -> 55.2 us
  waiting for transfers between devices: 48.5 us -> 46.8 us
    ppermute x28, starting transfers between devices: 51.1 us -> 46.1 us  [xor_swap(): return lax.ppermute(value, axis, [(i, i ^ by) for i in range(devices)])]
    ppermute x7 -> x13, starting transfers between devices: 3.56 us -> 6.51 us  [wave(): return lax.ppermute(value, ('seg', 'ctl'), wave_pairs(nseg, nctl, tick))]
    ppermute x7 -> x13, waiting for transfers between devices: 9.93 us -> 8.22 us  [wave(): return lax.ppermute(value, ('seg', 'ctl'), wave_pairs(nseg, nctl, tick))]
    pallas_call x13 -> x19, Pallas kernels: 6.28 us -> 7.12 us  [call(): pl.pallas_call(kernel, out_shape=outs, in_specs=[VMEM] * len(args), out_s...]
  transfers between devices with their start and end apart: 37 -> 43, of which waited for: 13 -> 13; matrix products, arithmetic and copies ran while one was open for 0% -> 0% of each run, Pallas kernels for 5% -> 6%
where the time goes in v3:
time: 114 us
  starting transfers between devices  55.2 us (48%)
  waiting for transfers between devices  46.8 us (41%)
  Pallas kernels  7.12 us (6%)
  local copies, waits for them, and re-layouts  3.71 us (3%)
    ppermute x28, starting transfers between devices, xor_swap(): return lax.ppermute(value, axis, [(i, i ^ by) for i in range(devices)])  46.1 us
    ppermute x28, waiting for transfers between devices, xor_swap(): return lax.ppermute(value, axis, [(i, i ^ by) for i in range(devices)])  30.5 us
    ppermute x13, waiting for transfers between devices, wave(): return lax.ppermute(value, ('seg', 'ctl'), wave_pairs(nseg, nctl, tick))  8.22 us
    ppermute x2, waiting for transfers between devices, local(): last.append(lax.ppermute(late[2 * i + part], ('seg', 'ctl'), pairs))  8.11 us
    pallas_call x19, Pallas kernels, call(): pl.pallas_call(kernel, out_shape=outs, in_specs=[VMEM] * len(args), out_s...  7.12 us
    ppermute x13, starting transfers between devices, wave(): return lax.ppermute(value, ('seg', 'ctl'), wave_pairs(nseg, nctl, tick))  6.51 us
    ppermute x2, starting transfers between devices, local(): last.append(lax.ppermute(late[2 * i + part], ('seg', 'ctl'), pairs))  2.57 us
  transfers between devices with their start and end apart: 43, of which 13 were waited for; matrix products, arithmetic and copies ran while one was open for 0% of the time, Pallas kernels for 6%

profile of v3, /device:TPU:0, one launch (start us, length us, event | category | flops | bytes accessed | tf_op | source)
XLA Modules:
  0.0 113.6 jit_solution(13609727871242113871)
XLA Ops:
  0.6 1.3 %constant_dynamic-slice_fusion = f32[1,1024,64]{2,1,0:T(8,128)S(1)} fusion(f32[1,1024,256]{2,1,0:T(8,128)} %param.4, s32[]{:T(128)S(6)} %select_n.3), kind=kLoop, calls=%fused_computation | loop fusion | bytes 524292 | tf_op jit(solution)/shard_map/dynamic_slice | solution.py:230
  2.2 3.0 %collective-permute-start = (f32[64,1024]{1,0:T(8,128)S(1)}, f32[64,1024]{1,0:T(8,128)S(1)}, u32[]{:S(2)}, u32[]{:S(2)}) collective-permute-start(f32[64,1024]{1,0:T(8,128)S(1)} %bitcast.10), channel_id=1, source_target_pairs={{0,4},{4,8},{8,12},{12,16},{16,20},{20,24},{24,28},{28,0},{1,5},{5... | collective-permute-start | bytes 786440 | tf_op jit(solution)/shard_map/ppermute | solution.py:239
  5.2 2.2 %copy-done = f32[1,1024,1024]{2,1,0:T(8,128)S(1)} copy-done((f32[1,1024,1024]{2,1,0:T(8,128)S(1)}, f32[1,1024,1024]{2,1,0:T(8,128)}, u32[]{:S(2)}) %copy-start) | copy-done | bytes 4194328
  7.4 1.6 %shard_map.50 = (bf16[1024,1024]{1,0:T(8,128)(2,1)S(1)}, bf16[1024,1024]{1,0:T(8,128)(2,1)S(1)}, f32[256,1024]{1,0:T(8,128)S(1)}) custom-call(f32[1024,1024]{1,0:T(8,128)S(1)} %bitcast.7, f32[1024,256]{1,0:T(8,128)S(1)} %bitcast.8), custom_call_target="tpu_custom_call" | custom-call | bytes 10485760 | tf_op jit(solution)/shard_map/pallas_call | solution.py:25
  9.0 5.6 %collective-permute-done.x_ref = f32[64,1024]{1,0:T(8,128)S(1)} collective-permute-done((f32[64,1024]{1,0:T(8,128)S(1)}, f32[64,1024]{1,0:T(8,128)S(1)}, u32[]{:S(2)}, u32[]{:S(2)}) %collective-permute-start) | collective-permute-done | bytes 262176 | tf_op jit(solution)/shard_map/ppermute | solution.py:239
  14.6 0.5 collective-permute-start.4
  15.1 0.8 collective-permute-done.5.x_ref
  16.1 0.3 collective-permute-start.9
  16.4 0.8 collective-permute-done.10.x_ref
  17.4 0.3 collective-permute-start.14
  17.8 0.8 collective-permute-done.15.x_ref
  18.8 0.3 collective-permute-start.19
  19.1 1.5 %collective-permute-start.2 = (f32[64,1024]{1,0:T(8,128)S(1)}, f32[64,1024]{1,0:T(8,128)S(1)}, u32[]{:S(2)}, u32[]{:S(2)}) collective-permute-start(f32[64,1024]{1,0:T(8,128)S(1)} %get-tuple-element.32.refs_0_), channel_id=1, source_target_pairs={{0,2},{1,3},{2,0},{3,1},{4,6},{5,7},{6,4},{7,5},{8,10},{9,11},{10,... | collective-permute-start | bytes 786440 | tf_op jit(solution)/shard_map/ppermute | solution.py:218
  20.6 0.5 collective-permute-start.7
  21.2 0.2 collective-permute-start.6
  21.4 1.5 %collective-permute-start.12 = (f32[64,1024]{1,0:T(8,128)S(1)}, f32[64,1024]{1,0:T(8,128)S(1)}, u32[]{:S(2)}, u32[]{:S(2)}) collective-permute-start(f32[64,1024]{1,0:T(8,128)S(1)} %get-tuple-element.37.refs_8_), channel_id=1, source_target_pairs={{0,2},{1,3},{2,0},{3,1},{4,6},{5,7},{6,4},{7,5},{8,10},{9,11},{10,... | collective-permute-start | bytes 786440 | tf_op jit(solution)/shard_map/ppermute | solution.py:218
  22.9 5.4 %collective-permute-done.2.refs_2_ = f32[64,1024]{1,0:T(8,128)S(1)} collective-permute-done((f32[64,1024]{1,0:T(8,128)S(1)}, f32[64,1024]{1,0:T(8,128)S(1)}, u32[]{:S(2)}, u32[]{:S(2)}) %collective-permute-start.2) | collective-permute-done | bytes 262176 | tf_op jit(solution)/shard_map/ppermute | solution.py:218
  28.3 0.5 collective-permute-start.25
  28.8 5.1 %collective-permute-done.7.refs_6_ = f32[64,1024]{1,0:T(8,128)S(1)} collective-permute-done((f32[64,1024]{1,0:T(8,128)S(1)}, f32[64,1024]{1,0:T(8,128)S(1)}, u32[]{:S(2)}, u32[]{:S(2)}) %collective-permute-start.7) | collective-permute-done | bytes 262176 | tf_op jit(solution)/shard_map/ppermute | solution.py:218
  33.9 0.5 collective-permute-start.24
  34.4 4.3 %collective-permute-done.12.refs_10_ = f32[64,1024]{1,0:T(8,128)S(1)} collective-permute-done((f32[64,1024]{1,0:T(8,128)S(1)}, f32[64,1024]{1,0:T(8,128)S(1)}, u32[]{:S(2)}, u32[]{:S(2)}) %collective-permute-start.12) | collective-permute-done | bytes 262176 | tf_op jit(solution)/shard_map/ppermute | solution.py:218
  38.8 1.5 %collective-permute-start.17 = (f32[64,1024]{1,0:T(8,128)S(1)}, f32[64,1024]{1,0:T(8,128)S(1)}, u32[]{:S(2)}, u32[]{:S(2)}) collective-permute-start(f32[64,1024]{1,0:T(8,128)S(1)} %get-tuple-element.39.refs_12_), channel_id=1, source_target_pairs={{0,2},{1,3},{2,0},{3,1},{4,6},{5,7},{6,4},{7,5},{8,10},{9,11},{10,... | collective-permute-start | bytes 786440 | tf_op jit(solution)/shard_map/ppermute | solution.py:218
  40.3 0.6 collective-permute-start.22
  41.0 0.3 collective-permute-start.29
  41.4 6.6 %collective-permute-done.17.refs_14_ = f32[64,1024]{1,0:T(8,128)S(1)} collective-permute-done((f32[64,1024]{1,0:T(8,128)S(1)}, f32[64,1024]{1,0:T(8,128)S(1)}, u32[]{:S(2)}, u32[]{:S(2)}) %collective-permute-start.17) | collective-permute-done | bytes 262176 | tf_op jit(solution)/shard_map/ppermute | solution.py:218
  47.9 0.5 collective-permute-start.21
  48.5 0.4 collective-permute-start.18
  49.0 2.9 %collective-permute-done.22.refs_18_.refs_2_ = f32[64,1024]{1,0:T(8,128)S(1)} collective-permute-done((f32[64,1024]{1,0:T(8,128)S(1)}, f32[64,1024]{1,0:T(8,128)S(1)}, u32[]{:S(2)}, u32[]{:S(2)}) %collective-permute-start.22) | collective-permute-done | bytes 262176 | tf_op jit(solution)/shard_map/ppermute | solution.py:218
  51.9 0.7 shard_map.63
  52.6 1.5 %collective-permute-start.27 = (f32[64,1024]{1,0:T(8,128)S(1)}, f32[64,1024]{1,0:T(8,128)S(1)}, u32[]{:S(2)}, u32[]{:S(2)}) collective-permute-start(f32[64,1024]{1,0:T(8,128)S(1)} %get-tuple-element.43.refs_20_.refs_4_), channel_id=1, source_target_pairs={{0,2},{1,3},{2,0},{3,1},{4,6},{5,7},{6,4},{7,5},{8,10},{9,11},{10,... | collective-permute-start | bytes 786440 | tf_op jit(solution)/shard_map/ppermute | solution.py:218
  54.1 0.5 collective-permute-start.32
  54.6 1.9 %shard_map.65 = (f32[64,512]{1,0:T(8,128)S(1)}, f32[64,512]{1,0:T(8,128)S(1)}, f32[64,512]{1,0:T(8,128)S(1)}, f32[64,512]{1,0:T(8,128)S(1)}, f32[64,512]{1,0:T(8...) custom-call(f32[1,1024]{1,0:T(1,128)S(1)} %copy-done.2, ...), custom_call_target="tpu_custom_call" | custom-call | flops 1610612736 | bytes 7344128 | tf_op jit(solution)/shard_map/pallas_call | solution.py:25
  56.6 7.8 %collective-permute-start.37 = (f32[64,512]{1,0:T(8,128)S(1)}, f32[64,512]{1,0:T(8,128)S(1)}, u32[]{:S(2)}, u32[]{:S(2)}) collective-permute-start(f32[64,512]{1,0:T(8,128)S(1)} %get-tuple-element.51), channel_id=1, source_target_pairs={{0,4},{4,0},{8,12},{12,8},{16,20},{20,16},{24,28},{28,24},{1,5},{5... | collective-permute-start | bytes 393224 | tf_op jit(solution)/shard_map/ppermute | solution.py:218
  64.4 14.2 %collective-permute-start.38 = (f32[64,512]{1,0:T(8,128)S(1)}, f32[64,512]{1,0:T(8,128)S(1)}, u32[]{:S(2)}, u32[]{:S(2)}) collective-permute-start(f32[64,512]{1,0:T(8,128)S(1)} %get-tuple-element.52), channel_id=1, source_target_pairs={{0,8},{4,12},{8,0},{12,4},{16,24},{20,28},{24,16},{28,20},{1,9},{5... | collective-permute-start | bytes 393224 | tf_op jit(solution)/shard_map/ppermute | solution.py:218
  78.6 0.5 collective-permute-start.31
  79.2 0.4 collective-permute-start.33
  79.6 2.3 %collective-permute-done.38.refs_2_ = f32[64,512]{1,0:T(8,128)S(1)} collective-permute-done((f32[64,512]{1,0:T(8,128)S(1)}, f32[64,512]{1,0:T(8,128)S(1)}, u32[]{:S(2)}, u32[]{:S(2)}) %collective-permute-start.38) | collective-permute-done | bytes 131104 | tf_op jit(solution)/shard_map/ppermute | solution.py:218
  81.9 6.9 %collective-permute-start.39 = (f32[64,512]{1,0:T(8,128)S(1)}, f32[64,512]{1,0:T(8,128)S(1)}, u32[]{:S(2)}, u32[]{:S(2)}) collective-permute-start(f32[64,512]{1,0:T(8,128)S(1)} %get-tuple-element.53), channel_id=1, source_target_pairs={{0,12},{4,8},{8,4},{12,0},{16,28},{20,24},{24,20},{28,16},{1,13},{... | collective-permute-start | bytes 393224 | tf_op jit(solution)/shard_map/ppermute | solution.py:218
  88.8 3.7 %collective-permute-done.39.refs_3_ = f32[64,512]{1,0:T(8,128)S(1)} collective-permute-done((f32[64,512]{1,0:T(8,128)S(1)}, f32[64,512]{1,0:T(8,128)S(1)}, u32[]{:S(2)}, u32[]{:S(2)}) %collective-permute-start.39) | collective-permute-done | bytes 131104 | tf_op jit(solution)/shard_map/ppermute | solution.py:218
  92.6 3.3 %collective-permute-start.35 = (f32[64,512]{1,0:T(8,128)S(1)}, f32[64,512]{1,0:T(8,128)S(1)}, u32[]{:S(2)}, u32[]{:S(2)}) collective-permute-start(f32[64,512]{1,0:T(8,128)S(1)} %get-tuple-element.48), channel_id=1, source_target_pairs={{0,8},{4,12},{8,0},{12,4},{16,24},{20,28},{24,16},{28,20},{1,9},{5... | collective-permute-start | bytes 393224 | tf_op jit(solution)/shard_map/ppermute | solution.py:218
  95.9 0.3 collective-permute-start.36
  96.2 3.7 %collective-permute-start.40 = (f32[64,512]{1,0:T(8,128)S(1)}, f32[64,512]{1,0:T(8,128)S(1)}, u32[]{:S(2)}, u32[]{:S(2)}) collective-permute-start(f32[64,512]{1,0:T(8,128)S(1)} %shard_map.66), channel_id=1, source_target_pairs={{0,16},{4,20},{8,24},{12,28},{16,0},{20,4},{24,8},{28,12},{1,17},{... | collective-permute-start | bytes 393224 | tf_op jit(solution)/shard_map/ppermute | solution.py:218
  99.9 1.3 %collective-permute-start.41 = (f32[64,512]{1,0:T(8,128)S(1)}, f32[64,512]{1,0:T(8,128)S(1)}, u32[]{:S(2)}, u32[]{:S(2)}) collective-permute-start(f32[64,512]{1,0:T(8,128)S(1)} %get-tuple-element.54), channel_id=1, source_target_pairs={{28,0},{24,16},{29,4},{25,20},{30,8},{26,24},{31,12},{27,28}} | collective-permute-start | bytes 393224 | tf_op jit(solution)/shard_map/ppermute | solution.py:312
  101.2 1.3 %collective-permute-start.42 = (f32[64,512]{1,0:T(8,128)S(1)}, f32[64,512]{1,0:T(8,128)S(1)}, u32[]{:S(2)}, u32[]{:S(2)}) collective-permute-start(f32[64,512]{1,0:T(8,128)S(1)} %get-tuple-element.55), channel_id=1, source_target_pairs={{28,16},{24,0},{29,20},{25,4},{30,24},{26,8},{31,28},{27,12}} | collective-permute-start | bytes 393224 | tf_op jit(solution)/shard_map/ppermute | solution.py:312
  102.5 2.2 %shard_map.64 = f32[1024,512]{1,0:T(8,128)} custom-call(f32[256,1024]{1,0:T(8,128)S(1)} %get-tuple-element.29.start_ref, f32[64,1024]{1,0:T(8,128)S(1)} %get-tuple-element.32.refs_0_, f32[64,1024]{1,0:T(8,128)S(1)} %collective-permute-done.1.refs_1_, f32[64,1024]{1,0:T(8,128)S(1)} %collective-permute-done.2.refs_2_, ...), custom_call_target="tpu_custom_call" | custom-call | bytes 10485760 | tf_op jit(solution)/shard_map/pallas_call | solution.py:25
  104.7 6.5 %collective-permute-done.41.refs_5_ = f32[64,512]{1,0:T(8,128)S(1)} collective-permute-done((f32[64,512]{1,0:T(8,128)S(1)}, f32[64,512]{1,0:T(8,128)S(1)}, u32[]{:S(2)}, u32[]{:S(2)}) %collective-permute-start.41) | collective-permute-done | bytes 131104 | tf_op jit(solution)/shard_map/ppermute | solution.py:312
  111.3 1.6 %collective-permute-done.42.refs_6_ = f32[64,512]{1,0:T(8,128)S(1)} collective-permute-done((f32[64,512]{1,0:T(8,128)S(1)}, f32[64,512]{1,0:T(8,128)S(1)}, u32[]{:S(2)}, u32[]{:S(2)}) %collective-permute-start.42) | collective-permute-done | bytes 131104 | tf_op jit(solution)/shard_map/ppermute | solution.py:312
  112.8 0.7 shard_map.68
  (65 shorter events, 1.2 us)
Async XLA Ops:
  0.6 4.6 %copy-start.1 = (f32[1,1024,256]{2,1,0:T(8,128)S(1)}, f32[1,1024,256]{2,1,0:T(8,128)}, u32[]{:S(2)}) copy-start(f32[1,1024,256]{2,1,0:T(8,128)} %param.4) | copy-start | bytes 3145732
  2.2 12.4 %collective-permute-start = (f32[64,1024]{1,0:T(8,128)S(1)}, f32[64,1024]{1,0:T(8,128)S(1)}, u32[]{:S(2)}, u32[]{:S(2)}) collective-permute-start(f32[64,1024]{1,0:T(8,128)S(1)} %bitcast.10), channel_id=1, source_target_pairs={{0,4},{4,8},{8,12},{12,16},{16,20},{20,24},{24,28},{28,0},{1,5},{5... | collective-permute-start | bytes 786440 | tf_op jit(solution)/shard_map/ppermute | solution.py:239
  5.2 2.2 %copy-start = (f32[1,1024,1024]{2,1,0:T(8,128)S(1)}, f32[1,1024,1024]{2,1,0:T(8,128)}, u32[]{:S(2)}) copy-start(f32[1,1024,1024]{2,1,0:T(8,128)} %param.3) | copy-start | bytes 12582916
  14.6 1.3 %collective-permute-start.5 = (f32[32,1024]{1,0:T(8,128)S(1)}, f32[32,1024]{1,0:T(8,128)S(1)}, u32[]{:S(2)}, u32[]{:S(2)}) collective-permute-start(f32[32,1024]{1,0:T(8,128)S(1)} %get-tuple-element.34), channel_id=1, source_target_pairs={{4,8},{8,12},{12,16},{16,20},{20,24},{24,28},{28,4},{0,1},{5,9},{9... | collective-permute-start | bytes 393224 | tf_op jit(solution)/shard_map/ppermute | solution.py:239
  14.6 1.5 %collective-permute-start.4 = (f32[32,1024]{1,0:T(8,128)S(1)}, f32[32,1024]{1,0:T(8,128)S(1)}, u32[]{:S(2)}, u32[]{:S(2)}) collective-permute-start(f32[32,1024]{1,0:T(8,128)S(1)} %get-tuple-element.33), channel_id=1, source_target_pairs={{4,8},{8,12},{12,16},{16,20},{20,24},{24,28},{28,4},{0,1},{5,9},{9... | collective-permute-start | bytes 393224 | tf_op jit(solution)/shard_map/ppermute | solution.py:239
  15.9 1.3 %collective-permute-start.10 = (f32[32,1024]{1,0:T(8,128)S(1)}, f32[32,1024]{1,0:T(8,128)S(1)}, u32[]{:S(2)}, u32[]{:S(2)}) collective-permute-start(f32[32,1024]{1,0:T(8,128)S(1)} %shard_map.52.refs_0_), channel_id=1, source_target_pairs={{8,12},{12,16},{16,20},{20,24},{24,28},{28,8},{0,1},{4,5},{9,13},{... | collective-permute-start | bytes 393224 | tf_op jit(solution)/shard_map/ppermute | solution.py:239
  16.1 1.3 %collective-permute-start.9 = (f32[32,1024]{1,0:T(8,128)S(1)}, f32[32,1024]{1,0:T(8,128)S(1)}, u32[]{:S(2)}, u32[]{:S(2)}) collective-permute-start(f32[32,1024]{1,0:T(8,128)S(1)} %get-tuple-element.36), channel_id=1, source_target_pairs={{8,12},{12,16},{16,20},{20,24},{24,28},{28,8},{0,1},{4,5},{9,13},{... | collective-permute-start | bytes 393224 | tf_op jit(solution)/shard_map/ppermute | solution.py:239
  17.3 1.3 %collective-permute-start.15 = (f32[32,1024]{1,0:T(8,128)S(1)}, f32[32,1024]{1,0:T(8,128)S(1)}, u32[]{:S(2)}, u32[]{:S(2)}) collective-permute-start(f32[32,1024]{1,0:T(8,128)S(1)} %shard_map.54.refs_0_), channel_id=1, source_target_pairs={{12,16},{16,20},{20,24},{24,28},{28,12},{0,1},{4,5},{8,9},{13,17},... | collective-permute-start | bytes 393224 | tf_op jit(solution)/shard_map/ppermute | solution.py:239
  17.4 1.3 %collective-permute-start.14 = (f32[32,1024]{1,0:T(8,128)S(1)}, f32[32,1024]{1,0:T(8,128)S(1)}, u32[]{:S(2)}, u32[]{:S(2)}) collective-permute-start(f32[32,1024]{1,0:T(8,128)S(1)} %get-tuple-element.38), channel_id=1, source_target_pairs={{12,16},{16,20},{20,24},{24,28},{28,12},{0,1},{4,5},{8,9},{13,17},... | collective-permute-start | bytes 393224 | tf_op jit(solution)/shard_map/ppermute | solution.py:239
  18.6 2.5 %collective-permute-start.20 = (f32[32,1024]{1,0:T(8,128)S(1)}, f32[32,1024]{1,0:T(8,128)S(1)}, u32[]{:S(2)}, u32[]{:S(2)}) collective-permute-start(f32[32,1024]{1,0:T(8,128)S(1)} %shard_map.56.refs_0_), channel_id=1, source_target_pairs={{16,20},{20,24},{24,28},{28,16},{0,1},{4,5},{8,9},{12,13},{17,21},... | collective-permute-start | bytes 393224 | tf_op jit(solution)/shard_map/ppermute | solution.py:239
  18.8 2.6 %collective-permute-start.19 = (f32[32,1024]{1,0:T(8,128)S(1)}, f32[32,1024]{1,0:T(8,128)S(1)}, u32[]{:S(2)}, u32[]{:S(2)}) collective-permute-start(f32[32,1024]{1,0:T(8,128)S(1)} %get-tuple-element.40), channel_id=1, source_target_pairs={{16,20},{20,24},{24,28},{28,16},{0,1},{4,5},{8,9},{12,13},{17,21},... | collective-permute-start | bytes 393224 | tf_op jit(solution)/shard_map/ppermute | solution.py:239
  19.1 9.2 %collective-permute-start.2 = (f32[64,1024]{1,0:T(8,128)S(1)}, f32[64,1024]{1,0:T(8,128)S(1)}, u32[]{:S(2)}, u32[]{:S(2)}) collective-permute-start(f32[64,1024]{1,0:T(8,128)S(1)} %get-tuple-element.32.refs_0_), channel_id=1, source_target_pairs={{0,2},{1,3},{2,0},{3,1},{4,6},{5,7},{6,4},{7,5},{8,10},{9,11},{10,... | collective-permute-start | bytes 786440 | tf_op jit(solution)/shard_map/ppermute | solution.py:218
  20.6 7.7 %collective-permute-start.1 = (f32[64,1024]{1,0:T(8,128)S(1)}, f32[64,1024]{1,0:T(8,128)S(1)}, u32[]{:S(2)}, u32[]{:S(2)}) collective-permute-start(f32[64,1024]{1,0:T(8,128)S(1)} %get-tuple-element.32.refs_0_), channel_id=1, source_target_pairs={{0,1},{1,0},{2,3},{3,2},{4,5},{5,4},{6,7},{7,6},{8,9},{9,8},{10,11... | collective-permute-start | bytes 786440 | tf_op jit(solution)/shard_map/ppermute | solution.py:218
  20.6 13.3 %collective-permute-start.7 = (f32[64,1024]{1,0:T(8,128)S(1)}, f32[64,1024]{1,0:T(8,128)S(1)}, u32[]{:S(2)}, u32[]{:S(2)}) collective-permute-start(f32[64,1024]{1,0:T(8,128)S(1)} %get-tuple-element.35.refs_4_), channel_id=1, source_target_pairs={{0,2},{1,3},{2,0},{3,1},{4,6},{5,7},{6,4},{7,5},{8,10},{9,11},{10,... | collective-permute-start | bytes 786440 | tf_op jit(solution)/shard_map/ppermute | solution.py:218
  21.2 12.8 %collective-permute-start.6 = (f32[64,1024]{1,0:T(8,128)S(1)}, f32[64,1024]{1,0:T(8,128)S(1)}, u32[]{:S(2)}, u32[]{:S(2)}) collective-permute-start(f32[64,1024]{1,0:T(8,128)S(1)} %get-tuple-element.35.refs_4_), channel_id=1, source_target_pairs={{0,1},{1,0},{2,3},{3,2},{4,5},{5,4},{6,7},{7,6},{8,9},{9,8},{10,11... | collective-permute-start | bytes 786440 | tf_op jit(solution)/shard_map/ppermute | solution.py:218
  21.4 17.4 %collective-permute-start.12 = (f32[64,1024]{1,0:T(8,128)S(1)}, f32[64,1024]{1,0:T(8,128)S(1)}, u32[]{:S(2)}, u32[]{:S(2)}) collective-permute-start(f32[64,1024]{1,0:T(8,128)S(1)} %get-tuple-element.37.refs_8_), channel_id=1, source_target_pairs={{0,2},{1,3},{2,0},{3,1},{4,6},{5,7},{6,4},{7,5},{8,10},{9,11},{10,... | collective-permute-start | bytes 786440 | tf_op jit(solution)/shard_map/ppermute | solution.py:218
  28.3 12.6 %collective-permute-start.11 = (f32[64,1024]{1,0:T(8,128)S(1)}, f32[64,1024]{1,0:T(8,128)S(1)}, u32[]{:S(2)}, u32[]{:S(2)}) collective-permute-start(f32[64,1024]{1,0:T(8,128)S(1)} %get-tuple-element.37.refs_8_), channel_id=1, source_target_pairs={{0,1},{1,0},{2,3},{3,2},{4,5},{5,4},{6,7},{7,6},{8,9},{9,8},{10,11... | collective-permute-start | bytes 786440 | tf_op jit(solution)/shard_map/ppermute | solution.py:218
  28.3 11.9 %collective-permute-start.25 = (f32[32,1024]{1,0:T(8,128)S(1)}, f32[32,1024]{1,0:T(8,128)S(1)}, u32[]{:S(2)}, u32[]{:S(2)}) collective-permute-start(f32[32,1024]{1,0:T(8,128)S(1)} %shard_map.58.refs_0_), channel_id=1, source_target_pairs={{20,24},{24,28},{28,20},{0,1},{4,5},{8,9},{12,13},{16,17},{21,25},... | collective-permute-start | bytes 393224 | tf_op jit(solution)/shard_map/ppermute | solution.py:239
  33.9 7.1 %collective-permute-start.3 = (f32[64,1024]{1,0:T(8,128)S(1)}, f32[64,1024]{1,0:T(8,128)S(1)}, u32[]{:S(2)}, u32[]{:S(2)}) collective-permute-start(f32[64,1024]{1,0:T(8,128)S(1)} %collective-permute-done.2.refs_2_), channel_id=1, source_target_pairs={{0,1},{1,0},{2,3},{3,2},{4,5},{5,4},{6,7},{7,6},{8,9},{9,8},{10,11... | collective-permute-start | bytes 786440 | tf_op jit(solution)/shard_map/ppermute | solution.py:218
  33.9 6.3 %collective-permute-start.24 = (f32[32,1024]{1,0:T(8,128)S(1)}, f32[32,1024]{1,0:T(8,128)S(1)}, u32[]{:S(2)}, u32[]{:S(2)}) collective-permute-start(f32[32,1024]{1,0:T(8,128)S(1)} %get-tuple-element.42), channel_id=1, source_target_pairs={{20,24},{24,28},{28,20},{0,1},{4,5},{8,9},{12,13},{16,17},{21,25},... | collective-permute-start | bytes 393224 | tf_op jit(solution)/shard_map/ppermute | solution.py:239
  38.8 9.2 %collective-permute-start.17 = (f32[64,1024]{1,0:T(8,128)S(1)}, f32[64,1024]{1,0:T(8,128)S(1)}, u32[]{:S(2)}, u32[]{:S(2)}) collective-permute-start(f32[64,1024]{1,0:T(8,128)S(1)} %get-tuple-element.39.refs_12_), channel_id=1, source_target_pairs={{0,2},{1,3},{2,0},{3,1},{4,6},{5,7},{6,4},{7,5},{8,10},{9,11},{10,... | collective-permute-start | bytes 786440 | tf_op jit(solution)/shard_map/ppermute | solution.py:218
  40.2 7.7 %collective-permute-start.16 = (f32[64,1024]{1,0:T(8,128)S(1)}, f32[64,1024]{1,0:T(8,128)S(1)}, u32[]{:S(2)}, u32[]{:S(2)}) collective-permute-start(f32[64,1024]{1,0:T(8,128)S(1)} %get-tuple-element.39.refs_12_), channel_id=1, source_target_pairs={{0,1},{1,0},{2,3},{3,2},{4,5},{5,4},{6,7},{7,6},{8,9},{9,8},{10,11... | collective-permute-start | bytes 786440 | tf_op jit(solution)/shard_map/ppermute | solution.py:218
  40.3 11.7 %collective-permute-start.22 = (f32[64,1024]{1,0:T(8,128)S(1)}, f32[64,1024]{1,0:T(8,128)S(1)}, u32[]{:S(2)}, u32[]{:S(2)}) collective-permute-start(f32[64,1024]{1,0:T(8,128)S(1)} %get-tuple-element.41.refs_16_.refs_0_), channel_id=1, source_target_pairs={{0,2},{1,3},{2,0},{3,1},{4,6},{5,7},{6,4},{7,5},{8,10},{9,11},{10,... | collective-permute-start | bytes 786440 | tf_op jit(solution)/shard_map/ppermute | solution.py:218
  40.9 7.6 %collective-permute-start.30 = (f32[32,1024]{1,0:T(8,128)S(1)}, f32[32,1024]{1,0:T(8,128)S(1)}, u32[]{:S(2)}, u32[]{:S(2)}) collective-permute-start(f32[32,1024]{1,0:T(8,128)S(1)} %shard_map.60.refs_0_), channel_id=1, source_target_pairs={{24,28},{28,24},{0,1},{4,5},{8,9},{12,13},{16,17},{20,21},{25,29},... | collective-permute-start | bytes 393224 | tf_op jit(solution)/shard_map/ppermute | solution.py:239
  41.0 7.5 %collective-permute-start.29 = (f32[32,1024]{1,0:T(8,128)S(1)}, f32[32,1024]{1,0:T(8,128)S(1)}, u32[]{:S(2)}, u32[]{:S(2)}) collective-permute-start(f32[32,1024]{1,0:T(8,128)S(1)} %get-tuple-element.44), channel_id=1, source_target_pairs={{24,28},{28,24},{0,1},{4,5},{8,9},{12,13},{16,17},{20,21},{25,29},... | collective-permute-start | bytes 393224 | tf_op jit(solution)/shard_map/ppermute | solution.py:239
  47.9 4.6 %collective-permute-start.8 = (f32[64,1024]{1,0:T(8,128)S(1)}, f32[64,1024]{1,0:T(8,128)S(1)}, u32[]{:S(2)}, u32[]{:S(2)}) collective-permute-start(f32[64,1024]{1,0:T(8,128)S(1)} %collective-permute-done.7.refs_6_), channel_id=1, source_target_pairs={{0,1},{1,0},{2,3},{3,2},{4,5},{5,4},{6,7},{7,6},{8,9},{9,8},{10,11... | collective-permute-start | bytes 786440 | tf_op jit(solution)/shard_map/ppermute | solution.py:218
  47.9 6.1 %collective-permute-start.21 = (f32[64,1024]{1,0:T(8,128)S(1)}, f32[64,1024]{1,0:T(8,128)S(1)}, u32[]{:S(2)}, u32[]{:S(2)}) collective-permute-start(f32[64,1024]{1,0:T(8,128)S(1)} %get-tuple-element.41.refs_16_.refs_0_), channel_id=1, source_target_pairs={{0,1},{1,0},{2,3},{3,2},{4,5},{5,4},{6,7},{7,6},{8,9},{9,8},{10,11... | collective-permute-start | bytes 786440 | tf_op jit(solution)/shard_map/ppermute | solution.py:218
  48.4 6.2 %collective-permute-start.13 = (f32[64,1024]{1,0:T(8,128)S(1)}, f32[64,1024]{1,0:T(8,128)S(1)}, u32[]{:S(2)}, u32[]{:S(2)}) collective-permute-start(f32[64,1024]{1,0:T(8,128)S(1)} %collective-permute-done.12.refs_10_), channel_id=1, source_target_pairs={{0,1},{1,0},{2,3},{3,2},{4,5},{5,4},{6,7},{7,6},{8,9},{9,8},{10,11... | collective-permute-start | bytes 786440 | tf_op jit(solution)/shard_map/ppermute | solution.py:218
  48.5 6.1 %collective-permute-start.18 = (f32[64,1024]{1,0:T(8,128)S(1)}, f32[64,1024]{1,0:T(8,128)S(1)}, u32[]{:S(2)}, u32[]{:S(2)}) collective-permute-start(f32[64,1024]{1,0:T(8,128)S(1)} %collective-permute-done.17.refs_14_), channel_id=1, source_target_pairs={{0,1},{1,0},{2,3},{3,2},{4,5},{5,4},{6,7},{7,6},{8,9},{9,8},{10,11... | collective-permute-start | bytes 786440 | tf_op jit(solution)/shard_map/ppermute | solution.py:218
  51.9 2.7 %collective-permute-start.23 = (f32[64,1024]{1,0:T(8,128)S(1)}, f32[64,1024]{1,0:T(8,128)S(1)}, u32[]{:S(2)}, u32[]{:S(2)}) collective-permute-start(f32[64,1024]{1,0:T(8,128)S(1)} %collective-permute-done.22.refs_18_.refs_2_), channel_id=1, source_target_pairs={{0,1},{1,0},{2,3},{3,2},{4,5},{5,4},{6,7},{7,6},{8,9},{9,8},{10,11... | collective-permute-start | bytes 786440 | tf_op jit(solution)/shard_map/ppermute | solution.py:218
  51.9 2.7 %copy-start.2 = (f32[1,1024]{1,0:T(1,128)S(1)}, f32[1,1024]{1,0:T(1,128)}, u32[]{:S(2)}) copy-start(f32[1,1024]{1,0:T(1,128)} %weight_ref.3) | copy-start | bytes 12292
  52.6 26.0 %collective-permute-start.27 = (f32[64,1024]{1,0:T(8,128)S(1)}, f32[64,1024]{1,0:T(8,128)S(1)}, u32[]{:S(2)}, u32[]{:S(2)}) collective-permute-start(f32[64,1024]{1,0:T(8,128)S(1)} %get-tuple-element.43.refs_20_.refs_4_), channel_id=1, source_target_pairs={{0,2},{1,3},{2,0},{3,1},{4,6},{5,7},{6,4},{7,5},{8,10},{9,11},{10,... | collective-permute-start | bytes 786440 | tf_op jit(solution)/shard_map/ppermute | solution.py:218
  54.1 25.1 %collective-permute-start.32 = (f32[64,1024]{1,0:T(8,128)S(1)}, f32[64,1024]{1,0:T(8,128)S(1)}, u32[]{:S(2)}, u32[]{:S(2)}) collective-permute-start(f32[64,1024]{1,0:T(8,128)S(1)} %get-tuple-element.45.refs_24_.refs_8_), channel_id=1, source_target_pairs={{0,2},{1,3},{2,0},{3,1},{4,6},{5,7},{6,4},{7,5},{8,10},{9,11},{10,... | collective-permute-start | bytes 786440 | tf_op jit(solution)/shard_map/ppermute | solution.py:218
  56.6 22.6 %collective-permute-start.37 = (f32[64,512]{1,0:T(8,128)S(1)}, f32[64,512]{1,0:T(8,128)S(1)}, u32[]{:S(2)}, u32[]{:S(2)}) collective-permute-start(f32[64,512]{1,0:T(8,128)S(1)} %get-tuple-element.51), channel_id=1, source_target_pairs={{0,4},{4,0},{8,12},{12,8},{16,20},{20,16},{24,28},{28,24},{1,5},{5... | collective-permute-start | bytes 393224 | tf_op jit(solution)/shard_map/ppermute | solution.py:218
  64.4 17.5 %collective-permute-start.38 = (f32[64,512]{1,0:T(8,128)S(1)}, f32[64,512]{1,0:T(8,128)S(1)}, u32[]{:S(2)}, u32[]{:S(2)}) collective-permute-start(f32[64,512]{1,0:T(8,128)S(1)} %get-tuple-element.52), channel_id=1, source_target_pairs={{0,8},{4,12},{8,0},{12,4},{16,24},{20,28},{24,16},{28,20},{1,9},{5... | collective-permute-start | bytes 393224 | tf_op jit(solution)/shard_map/ppermute | solution.py:218
  78.6 14.0 %collective-permute-start.26 = (f32[64,1024]{1,0:T(8,128)S(1)}, f32[64,1024]{1,0:T(8,128)S(1)}, u32[]{:S(2)}, u32[]{:S(2)}) collective-permute-start(f32[64,1024]{1,0:T(8,128)S(1)} %get-tuple-element.43.refs_20_.refs_4_), channel_id=1, source_target_pairs={{0,1},{1,0},{2,3},{3,2},{4,5},{5,4},{6,7},{7,6},{8,9},{9,8},{10,11... | collective-permute-start | bytes 786440 | tf_op jit(solution)/shard_map/ppermute | solution.py:218
  78.6 17.3 %collective-permute-start.31 = (f32[64,1024]{1,0:T(8,128)S(1)}, f32[64,1024]{1,0:T(8,128)S(1)}, u32[]{:S(2)}, u32[]{:S(2)}) collective-permute-start(f32[64,1024]{1,0:T(8,128)S(1)} %get-tuple-element.45.refs_24_.refs_8_), channel_id=1, source_target_pairs={{0,1},{1,0},{2,3},{3,2},{4,5},{5,4},{6,7},{7,6},{8,9},{9,8},{10,11... | collective-permute-start | bytes 786440 | tf_op jit(solution)/shard_map/ppermute | solution.py:218
  79.1 17.0 %collective-permute-start.28 = (f32[64,1024]{1,0:T(8,128)S(1)}, f32[64,1024]{1,0:T(8,128)S(1)}, u32[]{:S(2)}, u32[]{:S(2)}) collective-permute-start(f32[64,1024]{1,0:T(8,128)S(1)} %collective-permute-done.27.refs_22_.refs_6_), channel_id=1, source_target_pairs={{0,1},{1,0},{2,3},{3,2},{4,5},{5,4},{6,7},{7,6},{8,9},{9,8},{10,11... | collective-permute-start | bytes 786440 | tf_op jit(solution)/shard_map/ppermute | solution.py:218
  79.2 20.7 %collective-permute-start.33 = (f32[64,1024]{1,0:T(8,128)S(1)}, f32[64,1024]{1,0:T(8,128)S(1)}, u32[]{:S(2)}, u32[]{:S(2)}) collective-permute-start(f32[64,1024]{1,0:T(8,128)S(1)} %collective-permute-done.32.refs_26_.refs_10_), channel_id=1, source_target_pairs={{0,1},{1,0},{2,3},{3,2},{4,5},{5,4},{6,7},{7,6},{8,9},{9,8},{10,11... | collective-permute-start | bytes 786440 | tf_op jit(solution)/shard_map/ppermute | solution.py:218
  81.9 10.6 %collective-permute-start.39 = (f32[64,512]{1,0:T(8,128)S(1)}, f32[64,512]{1,0:T(8,128)S(1)}, u32[]{:S(2)}, u32[]{:S(2)}) collective-permute-start(f32[64,512]{1,0:T(8,128)S(1)} %get-tuple-element.53), channel_id=1, source_target_pairs={{0,12},{4,8},{8,4},{12,0},{16,28},{20,24},{24,20},{28,16},{1,13},{... | collective-permute-start | bytes 393224 | tf_op jit(solution)/shard_map/ppermute | solution.py:218
  92.6 8.6 %collective-permute-start.34 = (f32[64,512]{1,0:T(8,128)S(1)}, f32[64,512]{1,0:T(8,128)S(1)}, u32[]{:S(2)}, u32[]{:S(2)}) collective-permute-start(f32[64,512]{1,0:T(8,128)S(1)} %get-tuple-element.47), channel_id=1, source_target_pairs={{0,4},{4,0},{8,12},{12,8},{16,20},{20,16},{24,28},{28,24},{1,5},{5... | collective-permute-start | bytes 393224 | tf_op jit(solution)/shard_map/ppermute | solution.py:218
  92.6 12.1 %collective-permute-start.35 = (f32[64,512]{1,0:T(8,128)S(1)}, f32[64,512]{1,0:T(8,128)S(1)}, u32[]{:S(2)}, u32[]{:S(2)}) collective-permute-start(f32[64,512]{1,0:T(8,128)S(1)} %get-tuple-element.48), channel_id=1, source_target_pairs={{0,8},{4,12},{8,0},{12,4},{16,24},{20,28},{24,16},{28,20},{1,9},{5... | collective-permute-start | bytes 393224 | tf_op jit(solution)/shard_map/ppermute | solution.py:218
  95.9 8.8 %collective-permute-start.36 = (f32[64,512]{1,0:T(8,128)S(1)}, f32[64,512]{1,0:T(8,128)S(1)}, u32[]{:S(2)}, u32[]{:S(2)}) collective-permute-start(f32[64,512]{1,0:T(8,128)S(1)} %get-tuple-element.49), channel_id=1, source_target_pairs={{0,12},{4,8},{8,4},{12,0},{16,28},{20,24},{24,20},{28,16},{1,13},{... | collective-permute-start | bytes 393224 | tf_op jit(solution)/shard_map/ppermute | solution.py:218
  96.2 8.6 %collective-permute-start.40 = (f32[64,512]{1,0:T(8,128)S(1)}, f32[64,512]{1,0:T(8,128)S(1)}, u32[]{:S(2)}, u32[]{:S(2)}) collective-permute-start(f32[64,512]{1,0:T(8,128)S(1)} %shard_map.66), channel_id=1, source_target_pairs={{0,16},{4,20},{8,24},{12,28},{16,0},{20,4},{24,8},{28,12},{1,17},{... | collective-permute-start | bytes 393224 | tf_op jit(solution)/shard_map/ppermute | solution.py:218
  99.9 11.4 %collective-permute-start.41 = (f32[64,512]{1,0:T(8,128)S(1)}, f32[64,512]{1,0:T(8,128)S(1)}, u32[]{:S(2)}, u32[]{:S(2)}) collective-permute-start(f32[64,512]{1,0:T(8,128)S(1)} %get-tuple-element.54), channel_id=1, source_target_pairs={{28,0},{24,16},{29,4},{25,20},{30,8},{26,24},{31,12},{27,28}} | collective-permute-start | bytes 393224 | tf_op jit(solution)/shard_map/ppermute | solution.py:312
  101.2 11.7 %collective-permute-start.42 = (f32[64,512]{1,0:T(8,128)S(1)}, f32[64,512]{1,0:T(8,128)S(1)}, u32[]{:S(2)}, u32[]{:S(2)}) collective-permute-start(f32[64,512]{1,0:T(8,128)S(1)} %get-tuple-element.55), channel_id=1, source_target_pairs={{28,16},{24,0},{29,20},{25,4},{30,24},{26,8},{31,28},{27,12}} | collective-permute-start | bytes 393224 | tf_op jit(solution)/shard_map/ppermute | solution.py:312
